TPU v7x, 512 devices: a whole 4x8x8 slice. The times are simulated.
512 devices in a mesh: tm: 16 (over x, z_hi, core), coef: 32 (over y, z_lo).
Axes of the slice: x: 4, y: 8, z: 8 (z_hi: 2, z_lo: 4; z = z_hi * 4 + z_lo), core: 2. Of those that a mesh axis runs over, the one named last changes fastest.
Arguments:
- design: float32 [8192, 40960], P('tm', 'coef'), may hold values from -4 to 4
- whitening: float32 [8192, 256], P('tm'), may hold values from -1 to 3, as said below
- solution: float32 [40960, 64], P('coef'), may hold values from -6 to 6
- direction: float32 [40960, 64], P('coef'), may hold values from -6 to 6
- gradient_prev: float32 [40960, 64], P('coef'), may hold values from -25 to 25
- residual: float32 [8192, 64], P('tm'), may hold values from -6 to 6
Outputs:
- new_solution: float32 [40960, 64], P('coef')
- new_residual: float32 [8192, 64], P('tm')
- new_direction: float32 [40960, 64], P('coef')
Inputs may be any that keep to these rules, and one draw needn't show every extreme that they name: `whitening`: the first tap of every row is positive.
All inputs are finite; a program needn't handle non-finite values.
Results may differ from a plain program's by a relative error of at most 0.00008.
Values sent between devices are 32-bit elements; how exact they have to be, the bound alone decides.
No kernel may reach another device: no remote copies, remote signals or barrier semaphores. Data moves between devices by JAX's collectives and lax.ppermute only.
A program may use at most 64 MiB of HBM per device.

v0:
```python
import jax
import jax.numpy as jnp
from jax import lax
from jax.sharding import PartitionSpec as P


def shifted(array, axis, by):
    devices = lax.axis_size(axis)
    pairs = [(i, i + by) for i in range(devices) if 0 <= i + by < devices]
    return lax.ppermute(array, axis, pairs)


def skewed_band(whitening):
    count, width = whitening.shape
    flipped = whitening[:, ::-1]
    padded = jnp.concatenate([flipped, jnp.zeros((count, count), whitening.dtype)], axis=1)
    return padded.reshape(-1)[: count * (count + width - 1)].reshape(count, count + width - 1)


def band_blocks(whitening):
    count, width = whitening.shape
    nblocks = count // width
    skewed = jax.vmap(skewed_band)(whitening.reshape(nblocks, width, width))
    return jnp.concatenate([skewed, jnp.zeros((nblocks, width, 1), jnp.float32)], axis=2)


def band_apply(blocks_band, extended):
    nblocks, width = (blocks_band.shape[0], blocks_band.shape[1])
    columns = extended.shape[1]
    padded = jnp.concatenate([extended, jnp.zeros((1, columns), jnp.float32)], axis=0)
    stacked = padded.reshape(nblocks + 1, width, columns)
    windows = jnp.concatenate([stacked[:-1], stacked[1:]], axis=1)
    result = jnp.einsum(
        "brj,bjc->brc",
        blocks_band,
        windows,
        precision=lax.Precision.HIGHEST,
        preferred_element_type=jnp.float32,
    )
    return result.reshape(nblocks * width, columns)


def band_adjoint(blocks_band, values):
    nblocks, width = (blocks_band.shape[0], blocks_band.shape[1])
    columns = values.shape[1]
    pieces = jnp.einsum(
        "brj,brc->bjc",
        blocks_band,
        values.reshape(nblocks, width, columns),
        precision=lax.Precision.HIGHEST,
        preferred_element_type=jnp.float32,
    )
    zero_block = jnp.zeros((1, width, columns), jnp.float32)
    total = jnp.concatenate([pieces[:, :width], zero_block], axis=0) + jnp.concatenate(
        [zero_block, pieces[:, width:]], axis=0
    )
    return total.reshape(-1, columns)[: nblocks * width + width - 1]


def product(left, right):
    return jnp.dot(left, right, precision=lax.Precision.HIGHEST, preferred_element_type=jnp.float32)


def product_left_t(left, right):
    return lax.dot_general(
        left,
        right,
        (((0,), (0,)), ((), ())),
        precision=lax.Precision.HIGHEST,
        preferred_element_type=jnp.float32,
    )


def per_device(design, whitening, solution, direction, gradient_prev, residual):
    count, width = whitening.shape
    rim_rows = width - 1
    banded = band_blocks(whitening)
    old_part = jnp.sum(gradient_prev * gradient_prev, axis=0)
    partial_value = product(design, direction)
    totals, old_norm = lax.psum((partial_value, old_part), "coef")
    pred_edge = shifted(totals[count - rim_rows :], "tm", 1)
    predicted = band_apply(banded, jnp.concatenate([pred_edge, totals], axis=0))
    energy = lax.psum(jnp.sum(predicted * predicted, axis=0), "tm")
    step_size = old_norm / energy
    new_solution = solution + step_size * direction
    new_residual = residual - step_size * predicted
    spread = band_adjoint(banded, new_residual)
    carried = shifted(spread[:rim_rows], "tm", -1)
    filler = jnp.zeros((count - rim_rows, spread.shape[1]), jnp.float32)
    whitened = spread[rim_rows:] + jnp.concatenate([filler, carried], axis=0)
    grad_part = product_left_t(design, whitened)
    gradient = lax.psum(grad_part, "tm")
    new_norm = lax.psum(jnp.sum(gradient * gradient, axis=0), "coef")
    new_direction = gradient + new_norm / old_norm * direction
    return (new_solution, new_residual, new_direction)


def solution(mesh):
    return jax.shard_map(
        per_device,
        mesh=mesh,
        in_specs=(
            P("tm", "coef"),
            P("tm", None),
            P("coef", None),
            P("coef", None),
            P("coef", None),
            P("tm", None),
        ),
        out_specs=(P("coef", None), P("tm", None), P("coef", None)),
        check_vma=False,
    )
```

profile of v0, /device:TPU:1, one launch (start us, length us, event | category | flops | bytes accessed | tf_op | source)
XLA Modules:
  0.0 691.9 jit_solution(8695370677998654144)
XLA Ops:
  7.2 0.0 copy-start
  7.2 0.0 all-reduce.9.cloned.1.call-start
  7.2 1.7 copy-done
  8.9 4.3 fusion.15
  13.2 0.0 all-reduce.9.cloned.1.call-update
  13.2 0.0 all-reduce.11.cloned.1.call-start
  13.3 3.8 rev.3
  17.1 0.1 pad_bitcast_fusion
  17.2 0.8 copy.22
  18.0 0.0 copy-start.3
  18.0 1.1 slice.45
  19.1 0.0 copy-start.5
  19.1 3.4 reshape.31
  22.6 266.3 %all-reduce.9.cloned.1.call-done = f32[512,64]{0,1:T(8,128)} async-done(((f32[512,64]{0,1:T(8,128)}), f32[512,64]{0,1:T(8,128)}) %all-reduce.9.cloned.1.call-update) | async-done | bytes 131088 | tf_op jit(solution)/shard_map/psum | solution.py:80
  288.9 0.9 slice.46
  289.8 23.3 %collective-permute-start = (f32[255,64]{0,1:T(8,128)S(1)}, f32[255,64]{0,1:T(8,128)S(1)}, u32[]{:S(2)}, u32[]{:S(2)}) collective-permute-start(f32[255,64]{0,1:T(8,128)S(1)} %slice.46), channel_id=1, source_target_pairs={{0,32},{32,64},{64,96},{96,128},{128,160},{160,192},{192,224},{224... | collective-permute-start | bytes 195848 | tf_op jit(solution)/shard_map/ppermute | solution.py:10
  313.1 0.0 copy-done.3
  313.1 0.1 multiply_reduce_fusion.1
  313.2 63.5 %psum.35 = f32[64]{0:T(128)S(1)} all-reduce(f32[64]{0:T(128)S(1)} %multiply_reduce_fusion.1), channel_id=1, replica_groups=mesh['tm'=16,'coef'=32] {'coef'}, use_global_device_ids=true, to_apply=%region_1.0 | all-reduce | flops 64 | bytes 512 | tf_op jit(solution)/shard_map/psum | solution.py:80
  376.8 0.0 collective-permute-done
  376.8 1.1 pad_maximum_fusion
  377.9 2.5 multiply_reduce_fusion.2
  380.4 52.1 %psum.37 = f32[64]{0:T(128)S(1)} all-reduce(f32[64]{0:T(128)S(1)} %get-tuple-element.9), channel_id=1, replica_groups=mesh['tm'=16,'coef'=32] {'tm'}, use_global_device_ids=true, to_apply=%region_4.0 | all-reduce | flops 64 | bytes 512 | tf_op jit(solution)/shard_map/psum | solution.py:83
  432.5 0.0 copy-done.5
  432.5 0.1 multiply_subtract_fusion
  432.6 0.0 copy-start.2
  432.6 2.1 fusion
  434.7 0.0 copy-start.1
  434.7 0.0 copy-start.4
  434.8 2.7 collective-permute-start.1
  437.5 6.9 collective-permute-done.1
  444.4 2.4 convolution_bitcast_fusion
  446.8 0.0 copy-done.2
  446.8 0.0 all-reduce.11.cloned.1.call-update
  446.8 171.8 %all-reduce.11.cloned.1.call-done = f32[1280,64]{0,1:T(8,128)} async-done(((f32[1280,64]{0,1:T(8,128)}), f32[1280,64]{0,1:T(8,128)}) %all-reduce.11.cloned.1.call-update) | async-done | bytes 327696 | tf_op jit(solution)/shard_map/psum | solution.py:92
  618.6 1.1 multiply_reduce_fusion
  619.7 63.5 %psum.39 = f32[64]{0:T(128)S(1)} all-reduce(f32[64]{0:T(128)S(1)} %multiply_reduce_fusion), channel_id=1, replica_groups=mesh['tm'=16,'coef'=32] {'coef'}, use_global_device_ids=true, to_apply=%region_7.0 | all-reduce | flops 64 | bytes 512 | tf_op jit(solution)/shard_map/psum | solution.py:93
  683.2 0.0 copy-done.1
  683.2 0.0 copy-done.4
  683.2 1.9 multiply_add_fusion
  (8 shorter events, 0.1 us)
Async XLA Ops:
  7.2 1.7 copy-start
  7.2 281.7 %all-reduce.9.cloned.1.call-start = ((), (), s32[]{:S(2)}) async-start(), calls=%async_computation | async-start | bytes 262144 | tf_op jit(solution)/shard_map/psum | solution.py:80
  13.2 605.4 %all-reduce.11.cloned.1.call-start = ((), (), s32[]{:S(2)}) async-start(), calls=%async_computation.1 | async-start | bytes 655360 | tf_op jit(solution)/shard_map/psum | solution.py:92
  18.0 295.1 %copy-start.3 = (f32[1280,64]{0,1:T(8,128)S(1)}, f32[1280,64]{0,1:T(8,128)}, u32[]{:S(2)}) copy-start(f32[1280,64]{0,1:T(8,128)} %param.10) | copy-start | bytes 983044
  19.1 413.4 %copy-start.5 = (f32[512,64]{0,1:T(8,128)S(1)}, f32[512,64]{0,1:T(8,128)}, u32[]{:S(2)}) copy-start(f32[512,64]{0,1:T(8,128)} %param.11) | copy-start | bytes 393220
  289.8 87.0 %collective-permute-start = (f32[255,64]{0,1:T(8,128)S(1)}, f32[255,64]{0,1:T(8,128)S(1)}, u32[]{:S(2)}, u32[]{:S(2)}) collective-permute-start(f32[255,64]{0,1:T(8,128)S(1)} %slice.46), channel_id=1, source_target_pairs={{0,32},{32,64},{64,96},{96,128},{128,160},{160,192},{192,224},{224... | collective-permute-start | bytes 195848 | tf_op jit(solution)/shard_map/ppermute | solution.py:10
  432.6 14.2 %copy-start.2 = (f32[512,64]{0,1:T(8,128)}, f32[512,64]{0,1:T(8,128)S(1)}, u32[]{:S(2)}) copy-start(f32[512,64]{0,1:T(8,128)S(1)} %multiply_subtract_fusion) | copy-start | bytes 393220
  434.7 248.5 %copy-start.1 = (f32[1280,64]{0,1:T(8,128)S(1)}, f32[1280,64]{0,1:T(8,128)}, u32[]{:S(2)}) copy-start(f32[1280,64]{0,1:T(8,128)} %param.9) | copy-start | bytes 983044
  434.7 248.5 %copy-start.4 = (f32[1280,64]{0,1:T(8,128)S(1)}, f32[1280,64]{0,1:T(8,128)}, u32[]{:S(2)}) copy-start(f32[1280,64]{0,1:T(8,128)} %param.8) | copy-start | bytes 983044
  434.8 9.6 %collective-permute-start.1 = (f32[255,64]{0,1:T(8,128)S(1)}, f32[255,64]{0,1:T(8,128)S(1)}, u32[]{:S(2)}, u32[]{:S(2)}) collective-permute-start(f32[255,64]{0,1:T(8,128)S(1)} %slice.50), channel_id=1, source_target_pairs={{32,0},{64,32},{96,64},{128,96},{160,128},{192,160},{224,192},{256... | collective-permute-start | bytes 195848 | tf_op jit(solution)/shard_map/ppermute | solution.py:10
Sparse Core Ops, SparseCore 0:
  13.3 275.4 all-reduce.8
  446.9 171.5 all-reduce.10
where the time goes:
time: 705 us; the launch traced here: 692 us
  waiting for transfers between devices  445 us (63%)
  blocking collectives  179 us (25%)
  starting transfers between devices  26.1 us (4%)
  between operations  14.2 us (2%)
  local copies, waits for them, and re-layouts  12 us (2%)
  matrix products  11.2 us (2%)
    psum x1, waiting for transfers between devices, per_device(): totals, old_norm = lax.psum((partial_value, old_part), 'coef')  266 us
    psum x1, waiting for transfers between devices, per_device(): gradient = lax.psum(grad_part, 'tm')  172 us
    psum x1, blocking collectives, per_device(): totals, old_norm = lax.psum((partial_value, old_part), 'coef')  63.5 us
    psum x1, blocking collectives, per_device(): new_norm = lax.psum(jnp.sum(gradient * gradient, axis=0), 'coef')  63.5 us
    psum x1, blocking collectives, per_device(): energy = lax.psum(jnp.sum(predicted * predicted, axis=0), 'tm')  52.1 us
    ppermute x2, starting transfers between devices, shifted(): return lax.ppermute(array, axis, pairs)  26 us
  transfers between devices with their start and end apart: 4, of which 3 were waited for; matrix products, arithmetic and copies ran while one was open for 1% of the time, Pallas kernels for 0%

commit v1 on v0

v1 whole, which is shorter than its diff:
```python
import jax
import jax.numpy as jnp
from jax import lax
from jax.experimental import pallas as pl
from jax.experimental.pallas import tpu as pltpu
from jax.sharding import PartitionSpec as P

HIGHEST = lax.Precision.HIGHEST
BLOCK = 256


def dot_nn(a, b):
    return lax.dot_general(a, b, (((1,), (0,)), ((), ())), precision=HIGHEST, preferred_element_type=jnp.float32)


def dot_nt(a, b):
    return lax.dot_general(a, b, (((1,), (1,)), ((), ())), precision=HIGHEST, preferred_element_type=jnp.float32)


def skew(rows):
    return pltpu.roll(rows, 0, 1, stride=1, stride_axis=0)


def row_sums(values):
    padded = jnp.concatenate([values, jnp.zeros_like(values)], axis=0)
    return dot_nt(jnp.ones((8, values.shape[1]), jnp.float32), padded)


def as_column(row, first, count):
    shape = (count, 128)
    pick = lax.broadcasted_iota(jnp.int32, shape, 1) == lax.broadcasted_iota(jnp.int32, shape, 0) + first
    return jnp.sum(jnp.where(pick, jnp.broadcast_to(row[:1], shape), 0.0), axis=1, keepdims=True)


def predict_part(direction, design, gradient_prev):
    part = dot_nt(direction, design)
    tiles = [part[8 * j : 8 * j + 8, 128 * i : 128 * i + 128] for j in range(8) for i in range(4)]
    return jnp.stack(tiles), row_sums(gradient_prev * gradient_prev)


def band(whitening, rim, residual):
    taps = jnp.concatenate([whitening, rim[:BLOCK]], axis=0)
    lag = lax.broadcasted_iota(jnp.int32, (BLOCK, BLOCK), 0)
    lane = lax.broadcasted_iota(jnp.int32, (BLOCK, BLOCK), 1)
    mirror = jnp.where((lag + lane) % BLOCK == 0, 1.0, 0.0)
    mirrored = dot_nn(taps, mirror)
    same, before = [], []
    for b in range(3):
        full = skew(mirrored[BLOCK * b : BLOCK * (b + 1)])
        same.append(jnp.where(lane <= lag, full, 0.0))
        before.append(jnp.where(lane > lag, full, 0.0))
    res = [residual[:, :BLOCK], residual[:, BLOCK:], rim[BLOCK:]]
    back = [dot_nn(res[b], same[b]) + dot_nn(res[b + 1], before[b + 1]) for b in range(2)]
    return jnp.stack(same), jnp.stack(before), jnp.concatenate(back, axis=1)


def whiten_and_project(gathered, same, before, back, design):
    def block(halves, rows):
        return jnp.concatenate(
            [jnp.concatenate([gathered[4 * j + i][rows : rows + 8] for i in halves], axis=1) for j in range(8)], axis=0
        )

    plain = [block((2, 3), 8), block((0, 1), 0), block((2, 3), 0), block((0, 1), 8)]
    old = gathered[0][16:24]
    for m in range(1, 32):
        old = old + gathered[m][16:24]
    pred = [dot_nt(plain[b + 1], same[b]) + dot_nt(plain[b], before[b]) for b in range(3)]
    own = jnp.concatenate(pred[:2], axis=1)
    energy = row_sums(own * own)
    spread = [dot_nn(pred[b], same[b]) + dot_nn(pred[b + 1], before[b + 1]) for b in range(2)]
    both = jnp.concatenate([back, jnp.concatenate(spread, axis=1)], axis=0)
    grad = dot_nn(both, design)
    count = grad.shape[1] // 2
    pieces = []
    for j in range(8):
        for h in range(2):
            cut = slice(count * h, count * (h + 1))
            pieces.append(jnp.concatenate([grad[8 * j : 8 * j + 8, cut], grad[64 + 8 * j : 72 + 8 * j, cut], energy], axis=1))
    return jnp.stack(pieces), own, old


def step_piece(place, parts, old):
    total = parts[0]
    for m in range(1, parts.shape[0]):
        total = total + parts[m]
    count = (total.shape[1] - 128) // 2
    alpha = old / total[:, 2 * count :]
    alpha = jnp.where(lax.broadcasted_iota(jnp.int32, alpha.shape, 1) < 64, alpha, 0.0)
    grad = total[:, :count] - as_column(alpha, 8 * (place[0] // 2), 8) * total[:, count : 2 * count]
    return jnp.broadcast_to(grad[None], parts.shape[:1] + grad.shape), alpha


def assemble(pieces):
    return jnp.concatenate([jnp.concatenate([pieces[2 * j], pieces[2 * j + 1]], axis=1) for j in range(8)], axis=0)


def norm_part(pieces):
    grad = assemble(pieces)
    norm = row_sums(grad * grad)
    return jnp.broadcast_to(norm[None, :1], (32, 1, 128))


def finish(norms, pieces, old, alpha, solution, direction, residual, predicted):
    norm = norms[0]
    for m in range(1, norms.shape[0]):
        norm = norm + norms[m]
    step = as_column(alpha, 0, 64)
    beta = as_column(norm, 0, 64) / as_column(old, 0, 64)
    return (
        solution + step * direction,
        residual - step * predicted,
        assemble(pieces) + beta * direction,
    )


def run(function, outs, *args, scalar=False):
    def kernel(*refs):
        values = [refs[0] if scalar and k == 0 else r[...] for k, r in enumerate(refs[: len(args)])]
        results = function(*values)
        results = results if isinstance(results, tuple) else (results,)
        for ref, value in zip(refs[len(args) :], results, strict=True):
            ref[...] = value

    spaces = [pltpu.SMEM if scalar and k == 0 else pltpu.VMEM for k in range(len(args))]
    got = pl.pallas_call(
        kernel,
        out_shape=[jax.ShapeDtypeStruct(s, jnp.float32) for s in outs],
        in_specs=[pl.BlockSpec(memory_space=s) for s in spaces],
        out_specs=[pl.BlockSpec(memory_space=pltpu.VMEM) for _ in outs],
        name=function.__name__,
    )(*args)
    return got if len(outs) > 1 else got[0]


def exchange(array, axis):
    return lax.all_to_all(array, axis, 0, 0, tiled=True)


def per_device(design, whitening, solution, direction, gradient_prev, residual):
    blocks_t, blocks_c = lax.axis_size("tm"), lax.axis_size("coef")
    coefs = design.shape[1]
    solution, direction, gradient_prev, residual = solution.T, direction.T, gradient_prev.T, residual.T
    rim = lax.ppermute(
        jnp.concatenate([whitening[:BLOCK], residual[:, :BLOCK]], axis=0),
        "tm",
        [(i + 1, i) for i in range(blocks_t - 1)],
    )
    parts, old_part = run(predict_part, [(32, 8, 128), (8, 128)], direction, design, gradient_prev)
    tile = jnp.sum(exchange(parts, "coef"), axis=0)
    pairs = []
    for t in range(blocks_t):
        for c in range(blocks_c):
            to = t + 1 if c % 4 >= 2 else t - 1
            if 0 <= to < blocks_t:
                pairs.append((t * blocks_c + c, to * blocks_c + c))
    rim_tile = lax.ppermute(tile, ("tm", "coef"), pairs)
    same, before, back = run(
        band, [(3, BLOCK, BLOCK), (3, BLOCK, BLOCK), residual.shape], whitening, rim, residual
    )
    chunk = jnp.concatenate([tile, rim_tile, old_part], axis=0)
    gathered = exchange(jnp.broadcast_to(chunk[None], (blocks_c,) + chunk.shape), "coef")
    pieces, predicted, old = run(
        whiten_and_project,
        [(16, 8, coefs + 128), residual.shape, (8, 128)],
        gathered,
        same,
        before,
        back,
        design,
    )
    place = lax.axis_index("tm").astype(jnp.int32)[None]
    grad_piece, alpha = run(
        step_piece, [(16, 8, coefs // 2), (8, 128)], place, exchange(pieces, "tm"), old, scalar=True
    )
    pieces = exchange(grad_piece, "tm")
    norms = exchange(run(norm_part, [(32, 1, 128)], pieces), "coef")
    outs = run(
        finish,
        [solution.shape, residual.shape, direction.shape],
        norms,
        pieces,
        old,
        alpha,
        solution,
        direction,
        residual,
        predicted,
    )
    return tuple(out.T for out in outs)


def solution(mesh):
    return jax.shard_map(
        per_device,
        mesh=mesh,
        in_specs=(
            P("tm", "coef"),
            P("tm", None),
            P("coef", None),
            P("coef", None),
            P("coef", None),
            P("tm", None),
        ),
        out_specs=(P("coef", None), P("tm", None), P("coef", None)),
        check_vma=False,
    )
```

time: 705 us -> 151 us (0.21); the launches traced: 692 us -> 151 us
  waiting for transfers between devices: 445 us -> 40.8 us
  blocking collectives: 179 us -> 63.6 us
  Pallas kernels: 0 us -> 22.3 us
  between operations: 14.2 us -> 0.71 us
  matrix products: 11.2 us -> 0 us
  local copies, waits for them, and re-layouts: 12 us -> 3.13 us
    psum x2 -> x0, waiting for transfers between devices: 438 us -> none  [the longest x1 266 us: per_device(): totals, old_norm = lax.psum((partial_value, old_part), 'coef')]
    psum x3 -> x0, blocking collectives: 179 us -> none  [the longest x1 63.5 us: per_device(): totals, old_norm = lax.psum((partial_value, old_part), 'coef')]
    all_to_all x0 -> x3, blocking collectives: none -> 63.6 us  [exchange(): return lax.all_to_all(array, axis, 0, 0, tiled=True)]
    pallas_call x0 -> x6, Pallas kernels: none -> 22.3 us  [run(): pl.pallas_call(kernel, out_shape=[jax.ShapeDtypeStruct(s, jnp.float32) fo...]
    ppermute x2, starting transfers between devices: 26 us -> 5.88 us  [the longest x1 3.96 us: per_device(): rim_tile = lax.ppermute(tile, ('tm', 'coef'), pairs)]
    all_to_all x0 -> x2, waiting for transfers between devices: none -> 17.1 us  [exchange(): return lax.all_to_all(array, axis, 0, 0, tiled=True)]
    ppermute x2, waiting for transfers between devices: 6.91 us -> 23.7 us  [the longest x1 16.5 us: per_device(): lax.ppermute(jnp.concatenate([whitening[:BLOCK], residual[:, :BLOCK]], ax...]
    all_to_all x0 -> x2, starting transfers between devices: none -> 13.6 us  [exchange(): return lax.all_to_all(array, axis, 0, 0, tiled=True)]
  transfers between devices with their start and end apart: 4 -> 4, of which waited for: 3 -> 3; matrix products, arithmetic and copies ran while one was open for 1% -> 0% of each run, Pallas kernels for 0% -> 3%
where the time goes in v1:
time: 151 us
  blocking collectives  63.6 us (42%)
  waiting for transfers between devices  40.8 us (27%)
  Pallas kernels  22.3 us (15%)
  starting transfers between devices  19.4 us (13%)
  local copies, waits for them, and re-layouts  3.13 us (2%)
    all_to_all x3, blocking collectives, exchange(): return lax.all_to_all(array, axis, 0, 0, tiled=True)  63.6 us
    pallas_call x6, Pallas kernels, run(): pl.pallas_call(kernel, out_shape=[jax.ShapeDtypeStruct(s, jnp.float32) fo...  22.3 us
    all_to_all x2, waiting for transfers between devices, exchange(): return lax.all_to_all(array, axis, 0, 0, tiled=True)  17.1 us
    ppermute x1, waiting for transfers between devices, per_device(): lax.ppermute(jnp.concatenate([whitening[:BLOCK], residual[:, :BLOCK]], ax...  16.5 us
    all_to_all x2, starting transfers between devices, exchange(): return lax.all_to_all(array, axis, 0, 0, tiled=True)  13.6 us
    ppermute x1, waiting for transfers between devices, per_device(): rim_tile = lax.ppermute(tile, ('tm', 'coef'), pairs)  7.19 us
    ppermute x1, starting transfers between devices, per_device(): rim_tile = lax.ppermute(tile, ('tm', 'coef'), pairs)  3.96 us
  transfers between devices with their start and end apart: 4, of which 3 were waited for; matrix products, arithmetic and copies ran while one was open for 0% of the time, Pallas kernels for 3%

profile of v1, /device:TPU:1, one launch (start us, length us, event | category | flops | bytes accessed | tf_op | source)
XLA Modules:
  0.0 150.7 jit_solution(4975385749598134428)
XLA Ops:
  0.6 0.0 copy-start.2
  0.6 0.0 slice-start
  0.7 5.3 %predict_part.1 = (f32[32,8,128]{2,1,0:T(8,128)}, f32[8,128]{1,0:T(8,128)}) custom-call(f32[64,1280]{1,0:T(8,128)} %bitcast.8, f32[512,1280]{1,0:T(8,128)} %refs_4_.1, f32[64,1280]{1,0:T(8,128)} %bitcast.13), custom_call_target="tpu_custom_call" | custom-call | tf_op jit(solution)/shard_map/predict_part/pallas_call | solution.py:125
  6.0 23.4 %all_to_all.25 = f32[32,8,128]{2,1,0:T(8,128)S(1)} all-to-all(f32[32,8,128]{2,1,0:T(8,128)} %get-tuple-element.16), channel_id=1, replica_groups=mesh['tm'=16,'coef'=32] {'coef'}, dimensions={0} | all-to-all | bytes 262144 | tf_op jit(solution)/shard_map/all_to_all | solution.py:136
  29.4 4.0 %collective-permute-start = (f32[8,128]{1,0:T(8,128)S(1)}, f32[8,128]{1,0:T(8,128)S(1)}, u32[]{:S(2)}, u32[]{:S(2)}) collective-permute-start(f32[8,128]{1,0:T(8,128)S(1)} %reduce_sum.9), channel_id=1, source_target_pairs={{2,34},{3,35},{6,38},{7,39},{10,42},{11,43},{14,46},{15,47},{18,50... | collective-permute-start | bytes 12296 | tf_op jit(solution)/shard_map/ppermute | solution.py:156
  33.4 7.2 %collective-permute-done = f32[8,128]{1,0:T(8,128)S(1)} collective-permute-done((f32[8,128]{1,0:T(8,128)S(1)}, f32[8,128]{1,0:T(8,128)S(1)}, u32[]{:S(2)}, u32[]{:S(2)}) %collective-permute-start) | collective-permute-done | bytes 4128 | tf_op jit(solution)/shard_map/ppermute | solution.py:156
  40.6 0.7 pad_maximum_fusion.1
  41.2 0.8 broadcast_in_dim.10
  42.0 3.9 %all-to-all-start.1 = ((f32[32,24,128]{2,1,0:T(8,128)}), f32[32,24,128]{2,1,0:T(8,128)S(1)}, u32[]{:S(2)}, u32[]{:S(2)}) async-start(f32[32,24,128]{2,1,0:T(8,128)} %broadcast_in_dim.10), calls=%async_computation.1 | async-start | bytes 786432 | tf_op jit(solution)/shard_map/all_to_all | solution.py:136
  45.9 0.0 copy-done.2
  45.9 0.0 slice-done
  46.0 1.9 %collective-permute-start.1 = (f32[320,256]{1,0:T(8,128)S(1)}, f32[320,256]{1,0:T(8,128)S(1)}, u32[]{:S(2)}, u32[]{:S(2)}) collective-permute-start(f32[320,256]{1,0:T(8,128)S(1)} %pad_maximum_fusion), channel_id=1, source_target_pairs={{32,0},{64,32},{96,64},{128,96},{160,128},{192,160},{224,192},{256... | collective-permute-start | bytes 983048 | tf_op jit(solution)/shard_map/ppermute | solution.py:143
  47.9 16.5 %collective-permute-done.1.refs_1_ = f32[320,256]{1,0:T(8,128)S(1)} collective-permute-done((f32[320,256]{1,0:T(8,128)S(1)}, f32[320,256]{1,0:T(8,128)S(1)}, u32[]{:S(2)}, u32[]{:S(2)}) %collective-permute-start.1) | collective-permute-done | bytes 327712 | tf_op jit(solution)/shard_map/ppermute | solution.py:143
  64.4 0.0 copy-start.3
  64.4 0.7 copy-done.3
  65.1 4.0 %band.1 = (f32[3,256,256]{2,1,0:T(8,128)}, f32[3,256,256]{2,1,0:T(8,128)}, f32[64,512]{1,0:T(8,128)}) custom-call(f32[512,256]{1,0:T(8,128)} %refs_0_.1, f32[320,256]{1,0:T(8,128)} %copy-done.3, f32[64,512]{1,0:T(8,128)} %bitcast.10), custom_call_target="tpu_custom_call" | custom-call | tf_op jit(solution)/shard_map/band/pallas_call | solution.py:125
  69.1 0.0 all-to-all-done.1.refs_0_
  69.1 0.0 copy-start.1
  69.1 0.7 copy-done.1
  69.8 6.8 %whiten_and_project.1 = (f32[16,8,1408]{2,1,0:T(8,128)}, f32[64,512]{1,0:T(8,128)}, f32[8,128]{1,0:T(8,128)}) custom-call(f32[32,24,128]{2,1,0:T(8,128)} %copy-done.1, f32[3,256,256]{2,1,0:T(8,128)} %get-tuple-element.18.refs_1_, f32[3,256,256]{2,1,0:T(8,128)} %get-tuple-element.19.refs_2_, f32[64,512]{1,0:T(8,128)} %get-tuple-element.20.refs_3_, ...), custom_call_target="tpu_custom_call" | custom-call | tf_op jit(solution)/shard_map/whiten_and_project/pallas_call | solution.py:125
  76.6 9.7 %all-to-all-start.2 = ((f32[16,8,1408]{2,1,0:T(8,128)}), f32[16,8,1408]{2,1,0:T(8,128)S(1)}, u32[]{:S(2)}, u32[]{:S(2)}) async-start(f32[16,8,1408]{2,1,0:T(8,128)} %get-tuple-element.21), calls=%async_computation.2 | async-start | bytes 1441792 | tf_op jit(solution)/shard_map/all_to_all | solution.py:136
  86.3 17.1 %all-to-all-done.2.refs_1_ = f32[16,8,1408]{2,1,0:T(8,128)S(1)} async-done(((f32[16,8,1408]{2,1,0:T(8,128)}), f32[16,8,1408]{2,1,0:T(8,128)S(1)}, u32[]{:S(2)}, u32[]{:S(2)}) %all-to-all-start.2) | async-done | bytes 720928 | tf_op jit(solution)/shard_map/all_to_all | solution.py:136
  103.4 0.0 copy-start
  103.4 0.9 copy-done
  104.3 2.0 %step_piece.1 = (f32[16,8,640]{2,1,0:T(8,128)}, f32[8,128]{1,0:T(8,128)}) custom-call(s32[1]{0:T(128)} %bitcast.refs_0_, f32[16,8,1408]{2,1,0:T(8,128)} %copy-done, f32[8,128]{1,0:T(8,128)} %get-tuple-element.22.refs_2_), custom_call_target="tpu_custom_call" | custom-call | tf_op jit(solution)/shard_map/step_piece/pallas_call | solution.py:125
  106.2 16.6 %all_to_all.26.refs_0_.refs_1_ = f32[16,8,640]{2,1,0:T(8,128)} all-to-all(f32[16,8,640]{2,1,0:T(8,128)} %get-tuple-element.23), channel_id=1, replica_groups=mesh['tm'=16,'coef'=32] {'tm'}, dimensions={0} | all-to-all | bytes 655360 | tf_op jit(solution)/shard_map/all_to_all | solution.py:136
  122.9 2.0 %norm_part.1 = f32[32,1,128]{2,1,0:T(1,128)} custom-call(f32[16,8,640]{2,1,0:T(8,128)} %all_to_all.26.refs_0_.refs_1_), custom_call_target="tpu_custom_call" | custom-call | tf_op jit(solution)/shard_map/norm_part/pallas_call | solution.py:125
  124.8 23.6 %all_to_all.27.refs_0_ = f32[32,1,128]{2,1,0:T(1,128)} all-to-all(f32[32,1,128]{2,1,0:T(1,128)} %norm_part.1), channel_id=1, replica_groups=mesh['tm'=16,'coef'=32] {'coef'}, dimensions={0} | all-to-all | bytes 32768 | tf_op jit(solution)/shard_map/all_to_all | solution.py:136
  148.4 2.3 %finish.1 = (f32[64,1280]{1,0:T(8,128)}, f32[64,512]{1,0:T(8,128)}, f32[64,1280]{1,0:T(8,128)}) custom-call(f32[32,1,128]{2,1,0:T(1,128)} %all_to_all.27.refs_0_, f32[16,8,640]{2,1,0:T(8,128)} %all_to_all.26.refs_0_.refs_1_, f32[8,128]{1,0:T(8,128)} %get-tuple-element.22.refs_2_, f32[8,128]{1,0:T(8,128)} %get-tuple-element.24.refs_3_, f32[64,1280]{1,0:T(8,128)} %bitcast.14, ...), custom_call_target="tpu_custom_call" | custom-call | tf_op jit(solution)/shard_map/finish/pallas_call | solution.py:125
  (3 shorter events, 0.1 us)
Async XLA Ops:
  0.6 45.3 %copy-start.2 = (f32[512,64]{0,1:T(8,128)S(1)}, f32[512,64]{0,1:T(8,128)}, u32[]{:S(2)}) copy-start(f32[512,64]{0,1:T(8,128)} %param.11) | copy-start | bytes 393220
  0.6 45.3 %slice-start = ((f32[512,256]{1,0:T(8,128)}), f32[256,256]{1,0:T(8,128)S(1)}, s32[]{:S(2)}) async-start(f32[512,256]{1,0:T(8,128)} %refs_0_.1), calls=%async_computation.5 | async-start | bytes 524288 | tf_op jit(solution)/shard_map/slice | solution.py:144
  29.4 11.2 %collective-permute-start = (f32[8,128]{1,0:T(8,128)S(1)}, f32[8,128]{1,0:T(8,128)S(1)}, u32[]{:S(2)}, u32[]{:S(2)}) collective-permute-start(f32[8,128]{1,0:T(8,128)S(1)} %reduce_sum.9), channel_id=1, source_target_pairs={{2,34},{3,35},{6,38},{7,39},{10,42},{11,43},{14,46},{15,47},{18,50... | collective-permute-start | bytes 12296 | tf_op jit(solution)/shard_map/ppermute | solution.py:156
  42.0 27.1 %all-to-all-start.1 = ((f32[32,24,128]{2,1,0:T(8,128)}), f32[32,24,128]{2,1,0:T(8,128)S(1)}, u32[]{:S(2)}, u32[]{:S(2)}) async-start(f32[32,24,128]{2,1,0:T(8,128)} %broadcast_in_dim.10), calls=%async_computation.1 | async-start | bytes 786432 | tf_op jit(solution)/shard_map/all_to_all | solution.py:136
  46.0 18.4 %collective-permute-start.1 = (f32[320,256]{1,0:T(8,128)S(1)}, f32[320,256]{1,0:T(8,128)S(1)}, u32[]{:S(2)}, u32[]{:S(2)}) collective-permute-start(f32[320,256]{1,0:T(8,128)S(1)} %pad_maximum_fusion), channel_id=1, source_target_pairs={{32,0},{64,32},{96,64},{128,96},{160,128},{192,160},{224,192},{256... | collective-permute-start | bytes 983048 | tf_op jit(solution)/shard_map/ppermute | solution.py:143
  64.4 0.7 copy-start.3
  69.1 0.7 copy-start.1
  76.6 26.8 %all-to-all-start.2 = ((f32[16,8,1408]{2,1,0:T(8,128)}), f32[16,8,1408]{2,1,0:T(8,128)S(1)}, u32[]{:S(2)}, u32[]{:S(2)}) async-start(f32[16,8,1408]{2,1,0:T(8,128)} %get-tuple-element.21), calls=%async_computation.2 | async-start | bytes 1441792 | tf_op jit(solution)/shard_map/all_to_all | solution.py:136
  103.4 0.9 copy-start

commit v2 on v1

v2 whole, which is shorter than its diff:
```python
import jax
import jax.numpy as jnp
from jax import lax
from jax.experimental import pallas as pl
from jax.experimental.pallas import tpu as pltpu
from jax.sharding import PartitionSpec as P


HIGHEST = lax.Precision.HIGHEST
BLOCK = 256


def dot_nn(a, b):
    return lax.dot_general(a, b, (((1,), (0,)), ((), ())), precision=HIGHEST, preferred_element_type=jnp.float32)


def dot_nt(a, b):
    return lax.dot_general(a, b, (((1,), (1,)), ((), ())), precision=HIGHEST, preferred_element_type=jnp.float32)


def skew(rows):
    return pltpu.roll(rows, 0, 1, stride=1, stride_axis=0)


def row_sums(values):
    padded = jnp.concatenate([values, jnp.zeros_like(values)], axis=0)
    return dot_nt(jnp.ones((8, values.shape[1]), jnp.float32), padded)


def as_column(row, first, count):
    shape = (count, 128)
    pick = lax.broadcasted_iota(jnp.int32, shape, 1) == lax.broadcasted_iota(jnp.int32, shape, 0) + first
    return jnp.sum(jnp.where(pick, jnp.broadcast_to(row[:1], shape), 0.0), axis=1, keepdims=True)


def predict_part(direction, design, gradient_prev):
    part = dot_nt(direction, design)
    old = row_sums(gradient_prev * gradient_prev)[:1]
    rows = []
    for j in range(8):
        for i in range(4):
            rows += [part[8 * j : 8 * j + 8, 128 * i : 128 * i + 128], old]
    return jnp.concatenate(rows, axis=0)


def collect(rows):
    tile, old = rows[:8], rows[8:9]
    for m in range(1, 32):
        tile = tile + rows[9 * m : 9 * m + 8]
        old = old + rows[9 * m + 8 : 9 * m + 9]
    return tile, jnp.broadcast_to(old, (8, 128))


def chunk(tile, rim):
    return jnp.concatenate([tile, rim] * 32, axis=0)


def band(whitening, rim, residual, design):
    taps = jnp.concatenate([whitening, rim[:BLOCK]], axis=0)
    lag = lax.broadcasted_iota(jnp.int32, (BLOCK, BLOCK), 0)
    lane = lax.broadcasted_iota(jnp.int32, (BLOCK, BLOCK), 1)
    mirror = jnp.where((lag + lane) % BLOCK == 0, 1.0, 0.0)
    mirrored = dot_nn(taps, mirror)
    same, before = [], []
    for b in range(3):
        full = skew(mirrored[BLOCK * b : BLOCK * (b + 1)])
        same.append(jnp.where(lane <= lag, full, 0.0))
        before.append(jnp.where(lane > lag, full, 0.0))
    res = [residual[:, :BLOCK], residual[:, BLOCK:], rim[BLOCK:]]
    back = [dot_nn(res[b], same[b]) + dot_nn(res[b + 1], before[b + 1]) for b in range(2)]
    return jnp.stack(same), jnp.stack(before), dot_nn(jnp.concatenate(back, axis=1), design)


def whiten_and_project(gathered, same, before, back_grad, design):
    def block(halves, row):
        return jnp.concatenate(
            [
                jnp.concatenate([gathered[16 * m + row : 16 * m + row + 8] for m in (4 * j + i for i in halves)], axis=1)
                for j in range(8)
            ],
            axis=0,
        )

    plain = [block((2, 3), 8), block((0, 1), 0), block((2, 3), 0), block((0, 1), 8)]
    pred = [dot_nt(plain[b + 1], same[b]) + dot_nt(plain[b], before[b]) for b in range(3)]
    own = jnp.concatenate(pred[:2], axis=1)
    energy = row_sums(own * own)
    spread = [dot_nn(pred[b], same[b]) + dot_nn(pred[b + 1], before[b + 1]) for b in range(2)]
    grad = dot_nn(jnp.concatenate(spread, axis=1), design)
    return jnp.concatenate([back_grad, grad, jnp.concatenate([energy] * 8, axis=0)], axis=1), own


def sum_pieces(pieces):
    total = pieces[:8]
    for m in range(1, 8):
        total = total + pieces[8 * m : 8 * m + 8]
    return total


def step_piece(place, mine, other, old):
    total = mine + other
    count = (total.shape[1] - 128) // 2
    alpha = old / total[:, 2 * count :]
    alpha = jnp.where(lax.broadcasted_iota(jnp.int32, alpha.shape, 1) < 64, alpha, 0.0)
    grad = total[:, :count] - as_column(alpha, 8 * place[0], 8) * total[:, count : 2 * count]
    norm = jnp.sum(grad * grad, axis=1, keepdims=True)
    shape = (8, 128)
    pick = lax.broadcasted_iota(jnp.int32, shape, 0) == lax.broadcasted_iota(jnp.int32, shape, 1)
    row = jnp.sum(jnp.where(pick, jnp.broadcast_to(norm, shape), 0.0), axis=0, keepdims=True)
    return grad, alpha, jnp.broadcast_to(row, (32, 128))


def direction_piece(place, norms, grad, old, direction):
    norm = jnp.sum(norms, axis=0, keepdims=True)
    beta = as_column(norm, 0, 8) / as_column(old, 8 * place[0], 8)
    mine = direction[pl.ds(pl.multiple_of(8 * place[0], 8), 8), :]
    return jnp.concatenate([grad + beta * mine] * 8, axis=0)


def update(alpha, solution, direction, residual, predicted):
    step = as_column(alpha, 0, 64)
    return solution + step * direction, residual - step * predicted


def run(function, outs, *args, scalar=False, keep=()):
    def kernel(*refs):
        values = [r if k in keep else r[...] for k, r in enumerate(refs[: len(args)])]
        results = function(*values)
        results = results if isinstance(results, tuple) else (results,)
        for ref, value in zip(refs[len(args) :], results, strict=True):
            ref[...] = value

    spaces = [pltpu.SMEM if scalar and k == 0 else pltpu.VMEM for k in range(len(args))]
    got = pl.pallas_call(
        kernel,
        out_shape=[jax.ShapeDtypeStruct(s, jnp.float32) for s in outs],
        in_specs=[pl.BlockSpec(memory_space=s) for s in spaces],
        out_specs=[pl.BlockSpec(memory_space=pltpu.VMEM) for _ in outs],
    )(*args)
    return got if len(outs) > 1 else got[0]


def exchange(rows, axis, groups=None):
    return lax.all_to_all(rows, axis, 0, 0, axis_index_groups=groups, tiled=True)


def per_device(design, whitening, solution, direction, gradient_prev, residual):
    blocks_t, blocks_c = lax.axis_size("tm"), lax.axis_size("coef")
    coefs = design.shape[1]
    solution, direction, gradient_prev, residual = solution.T, direction.T, gradient_prev.T, residual.T
    groups = [[4 * x + 2 * z + k for x in range(4) for k in range(2)] for z in range(2)]
    t = lax.axis_index("tm").astype(jnp.int32)
    place = (lax.shift_right_logical(t, 2) * 2 + (t & 1))[None]
    rim = lax.ppermute(
        jnp.concatenate([whitening[:BLOCK], residual[:, :BLOCK]], axis=0),
        "tm",
        [(i + 1, i) for i in range(blocks_t - 1)],
    )
    rows = run(predict_part, [(9 * 32, 128)], direction, design, gradient_prev)
    rows = exchange(rows.reshape(32, 9 * 128), "coef").reshape(9 * 32, 128)
    same, before, back_grad = run(
        band,
        [(3, BLOCK, BLOCK), (3, BLOCK, BLOCK), (64, coefs)],
        whitening,
        rim,
        residual,
        design,
    )
    rows, same, before, back_grad = lax.optimization_barrier((rows, same, before, back_grad))
    tile, old = run(collect, [(8, 128), (8, 128)], rows)
    pairs = []
    for t in range(blocks_t):
        for c in range(blocks_c):
            to = t + 1 if c % 4 >= 2 else t - 1
            if 0 <= to < blocks_t:
                pairs.append((t * blocks_c + c, to * blocks_c + c))
    rim_tile = lax.ppermute(tile, ("tm", "coef"), pairs)
    gathered = exchange(run(chunk, [(16 * 32, 128)], tile, rim_tile), "coef")
    pieces, predicted = run(
        whiten_and_project,
        [(64, 2 * coefs + 128), residual.shape],
        gathered,
        same,
        before,
        back_grad,
        design,
    )
    mine = run(sum_pieces, [(8, 2 * coefs + 128)], exchange(pieces, "tm", groups))
    other = lax.ppermute(mine, "tm", [(i, i ^ 2) for i in range(blocks_t)])
    grad, alpha, norms = run(
        step_piece, [(8, coefs), (8, 128), (32, 128)], place, mine, other, old, scalar=True, keep=(0,)
    )
    norms = exchange(norms, "coef")
    new_solution, new_residual = run(
        update, [solution.shape, residual.shape], alpha, solution, direction, residual, predicted
    )
    pieces = run(
        direction_piece, [(64, coefs)], place, norms, grad, old, direction, scalar=True, keep=(0, 4)
    )
    return new_solution.T, new_residual.T, exchange(pieces, "tm", groups).T


def solution(mesh):
    return jax.shard_map(
        per_device,
        mesh=mesh,
        in_specs=(
            P("tm", "coef"),
            P("tm", None),
            P("coef", None),
            P("coef", None),
            P("coef", None),
            P("tm", None),
        ),
        out_specs=(P("coef", None), P("tm", None), P("coef", None)),
        check_vma=False,
    )
```

time: 151 us -> 140 us (0.927)
  waiting for transfers between devices: 40.8 us -> 24.7 us
  blocking collectives: 63.6 us -> 52.7 us
  starting transfers between devices: 19.4 us -> 27.3 us
  Pallas kernels: 22.3 us -> 28.8 us
  local copies, waits for them, and re-layouts: 3.13 us -> 5.15 us
    ppermute x1, waiting for transfers between devices: 16.5 us -> 0.01 us  [per_device(): lax.ppermute(jnp.concatenate([whitening[:BLOCK], residual[:, :BLOCK]], ax...]
    all_to_all x3, blocking collectives: 63.6 us -> 52.7 us  [exchange(): lax.all_to_all(rows, axis, 0, 0, axis_index_groups=groups, tiled=True)]
    all_to_all x2, waiting for transfers between devices: 17.1 us -> 9.42 us  [exchange(): lax.all_to_all(rows, axis, 0, 0, axis_index_groups=groups, tiled=True)]
    ppermute x0 -> x1, waiting for transfers between devices: none -> 7.58 us  [per_device(): other = lax.ppermute(mine, 'tm', [(i, i ^ 2) for i in range(blocks_t)])]
    ppermute x1, starting transfers between devices: 1.92 us -> 8.75 us  [per_device(): lax.ppermute(jnp.concatenate([whitening[:BLOCK], residual[:, :BLOCK]], ax...]
    pallas_call x6 -> x9, Pallas kernels: 22.3 us -> 28.8 us  [run(): pl.pallas_call(kernel, out_shape=[jax.ShapeDtypeStruct(s, jnp.float32) fo...]
    ppermute x0 -> x1, starting transfers between devices: none -> 3.03 us  [per_device(): other = lax.ppermute(mine, 'tm', [(i, i ^ 2) for i in range(blocks_t)])]
    ppermute x1, starting transfers between devices: 3.96 us -> 2.32 us  [per_device(): rim_tile = lax.ppermute(tile, ('tm', 'coef'), pairs)]
  transfers between devices with their start and end apart: 4 -> 5, of which waited for: 3 -> 4; matrix products, arithmetic and copies ran while one was open for 0% -> 0% of each run, Pallas kernels for 3% -> 10%
where the time goes in v2:
time: 140 us; the launch traced here: 139 us
  blocking collectives  52.7 us (38%)
  Pallas kernels  28.8 us (21%)
  starting transfers between devices  27.3 us (20%)
  waiting for transfers between devices  24.7 us (18%)
  local copies, waits for them, and re-layouts  5.15 us (4%)
    all_to_all x3, blocking collectives, exchange(): lax.all_to_all(rows, axis, 0, 0, axis_index_groups=groups, tiled=True)  52.7 us
    pallas_call x9, Pallas kernels, run(): pl.pallas_call(kernel, out_shape=[jax.ShapeDtypeStruct(s, jnp.float32) fo...  28.8 us
    all_to_all x2, starting transfers between devices, exchange(): lax.all_to_all(rows, axis, 0, 0, axis_index_groups=groups, tiled=True)  13.2 us
    all_to_all x2, waiting for transfers between devices, exchange(): lax.all_to_all(rows, axis, 0, 0, axis_index_groups=groups, tiled=True)  9.42 us
    ppermute x1, starting transfers between devices, per_device(): lax.ppermute(jnp.concatenate([whitening[:BLOCK], residual[:, :BLOCK]], ax...  8.75 us
    ppermute x1, waiting for transfers between devices, per_device(): rim_tile = lax.ppermute(tile, ('tm', 'coef'), pairs)  7.73 us
    ppermute x1, waiting for transfers between devices, per_device(): other = lax.ppermute(mine, 'tm', [(i, i ^ 2) for i in range(blocks_t)])  7.58 us
    unnamed x9, local copies, waits for them, and re-layouts  3.33 us
  transfers between devices with their start and end apart: 5, of which 4 were waited for; matrix products, arithmetic and copies ran while one was open for 0% of the time, Pallas kernels for 10%

profile of v2, /device:TPU:1, one launch (start us, length us, event | category | flops | bytes accessed | tf_op | source)
XLA Modules:
  0.0 139.5 jit_solution(3806300291121334938)
XLA Ops:
  0.6 0.8 slice.8
  1.5 1.0 slice.6
  2.5 8.7 %collective-permute-start = (f32[320,256]{1,0:T(8,128)S(1)}, f32[320,256]{1,0:T(8,128)S(1)}, u32[]{:S(2)}, u32[]{:S(2)}) collective-permute-start(f32[320,256]{1,0:T(8,128)S(1)} %pad_maximum_fusion), channel_id=1, source_target_pairs={{32,0},{64,32},{96,64},{128,96},{160,128},{192,160},{224,192},{256... | collective-permute-start | bytes 983048 | tf_op jit(solution)/shard_map/ppermute | solution.py:154
  11.2 5.3 %shard_map.85 = f32[288,128]{1,0:T(8,128)} custom-call(f32[64,1280]{1,0:T(8,128)} %bitcast.21, f32[512,1280]{1,0:T(8,128)} %refs_4_.1, f32[64,1280]{1,0:T(8,128)} %bitcast.36), custom_call_target="tpu_custom_call" | custom-call | tf_op jit(solution)/shard_map/pallas_call | solution.py:134
  16.5 7.3 %all-to-all-start = ((f32[32,1,1152]{2,1,0:T(1,128)}), f32[32,1,1152]{2,1,0:T(1,128)S(1)}, u32[]{:S(2)}, u32[]{:S(2)}) async-start(f32[32,1,1152]{2,1,0:T(1,128)} %bitcast.34), calls=%async_computation | async-start | bytes 294912 | tf_op jit(solution)/shard_map/all_to_all | solution.py:144
  23.8 0.0 collective-permute-done.refs_1_
  23.8 0.0 copy-start.1
  23.8 0.7 copy-done.1
  24.5 6.4 %shard_map.86 = (f32[3,256,256]{2,1,0:T(8,128)}, f32[3,256,256]{2,1,0:T(8,128)}, f32[64,1280]{1,0:T(8,128)}) custom-call(f32[512,256]{1,0:T(8,128)} %refs_0_.1, f32[320,256]{1,0:T(8,128)} %copy-done.1, f32[64,512]{1,0:T(8,128)} %bitcast.30, f32[512,1280]{1,0:T(8,128)} %refs_4_.1), custom_call_target="tpu_custom_call" | custom-call | tf_op jit(solution)/shard_map/pallas_call | solution.py:134
  31.0 4.4 %all-to-all-done = f32[32,1,1152]{2,1,0:T(1,128)S(1)} async-done(((f32[32,1,1152]{2,1,0:T(1,128)}), f32[32,1,1152]{2,1,0:T(1,128)S(1)}, u32[]{:S(2)}, u32[]{:S(2)}) %all-to-all-start) | async-done | bytes 147488 | tf_op jit(solution)/shard_map/all_to_all | solution.py:144
  35.3 0.0 copy-start
  35.3 0.7 copy-done
  36.0 1.5 %shard_map.87 = (f32[8,128]{1,0:T(8,128)}, f32[8,128]{1,0:T(8,128)}) custom-call(f32[288,128]{1,0:T(8,128)} %bitcast.33), custom_call_target="tpu_custom_call" | custom-call | tf_op jit(solution)/shard_map/pallas_call | solution.py:134
  37.5 2.3 %collective-permute-start.1 = (f32[8,128]{1,0:T(8,128)}, f32[8,128]{1,0:T(8,128)S(1)}, u32[]{:S(2)}, u32[]{:S(2)}) collective-permute-start(f32[8,128]{1,0:T(8,128)} %get-tuple-element.23.refs_0_), channel_id=1, source_target_pairs={{2,34},{3,35},{6,38},{7,39},{10,42},{11,43},{14,46},{15,47},{18,50... | collective-permute-start | bytes 12296 | tf_op jit(solution)/shard_map/ppermute | solution.py:177
  39.9 7.7 %collective-permute-done.1.refs_1_ = f32[8,128]{1,0:T(8,128)S(1)} collective-permute-done((f32[8,128]{1,0:T(8,128)}, f32[8,128]{1,0:T(8,128)S(1)}, u32[]{:S(2)}, u32[]{:S(2)}) %collective-permute-start.1) | collective-permute-done | bytes 4128 | tf_op jit(solution)/shard_map/ppermute | solution.py:177
  47.6 0.0 copy-start.3
  47.6 0.6 copy-done.3
  48.2 1.4 %shard_map.88 = f32[512,128]{1,0:T(8,128)} custom-call(f32[8,128]{1,0:T(8,128)} %get-tuple-element.23.refs_0_, f32[8,128]{1,0:T(8,128)} %copy-done.3), custom_call_target="tpu_custom_call" | custom-call | tf_op jit(solution)/shard_map/pallas_call | solution.py:134
  49.6 15.3 %all_to_all.54 = f32[32,16,128]{2,1,0:T(8,128)} all-to-all(f32[32,16,128]{2,1,0:T(8,128)} %bitcast.28), channel_id=1, replica_groups=mesh['tm'=16,'coef'=32] {'coef'}, dimensions={0} | all-to-all | bytes 524288 | tf_op jit(solution)/shard_map/all_to_all | solution.py:144
  65.0 6.8 %shard_map.89 = (f32[64,2688]{1,0:T(8,128)}, f32[64,512]{1,0:T(8,128)}) custom-call(f32[512,128]{1,0:T(8,128)} %bitcast.27, f32[3,256,256]{2,1,0:T(8,128)} %get-tuple-element.24.refs_1_, f32[3,256,256]{2,1,0:T(8,128)} %get-tuple-element.25.refs_2_, f32[64,1280]{1,0:T(8,128)} %get-tuple-element.26.refs_3_, f32[512,1280]{1,0:T(8,128)} %refs_4_.1), custom_call_target="tpu_custom_call" | custom-call | tf_op jit(solution)/shard_map/pallas_call | solution.py:134
  71.7 24.1 %all_to_all.55 = f32[8,8,2688]{2,1,0:T(8,128)} all-to-all(f32[8,8,2688]{2,1,0:T(8,128)} %bitcast.32), channel_id=1, replica_groups={{0,32,128,160,256,288,384,416},{64,96,192,224,320,352,448,480},{1,33,12..., dimensions={0} | all-to-all | bytes 1376256 | tf_op jit(solution)/shard_map/all_to_all | solution.py:144
  95.8 1.8 %shard_map.90.refs_1_ = f32[8,2688]{1,0:T(8,128)} custom-call(f32[64,2688]{1,0:T(8,128)} %bitcast.24), custom_call_target="tpu_custom_call" | custom-call | tf_op jit(solution)/shard_map/pallas_call | solution.py:134
  97.6 3.0 %collective-permute-start.2 = (f32[8,2688]{1,0:T(8,128)}, f32[8,2688]{1,0:T(8,128)S(1)}, u32[]{:S(2)}, u32[]{:S(2)}) collective-permute-start(f32[8,2688]{1,0:T(8,128)} %shard_map.90.refs_1_), channel_id=1, source_target_pairs={{0,64},{32,96},{64,0},{96,32},{128,192},{160,224},{192,128},{224,1... | collective-permute-start | bytes 258056 | tf_op jit(solution)/shard_map/ppermute | solution.py:189
  100.7 7.6 %collective-permute-done.2.refs_2_ = f32[8,2688]{1,0:T(8,128)S(1)} collective-permute-done((f32[8,2688]{1,0:T(8,128)}, f32[8,2688]{1,0:T(8,128)S(1)}, u32[]{:S(2)}, u32[]{:S(2)}) %collective-permute-start.2) | collective-permute-done | bytes 86048 | tf_op jit(solution)/shard_map/ppermute | solution.py:189
  108.2 0.0 copy-start.2
  108.2 0.6 copy-done.2
  108.9 1.7 %shard_map.91 = (f32[8,1280]{1,0:T(8,128)}, f32[8,128]{1,0:T(8,128)}, f32[32,128]{1,0:T(8,128)}) custom-call(s32[1]{0:T(128)} %bitcast.refs_0_, f32[8,2688]{1,0:T(8,128)} %shard_map.90.refs_1_, f32[8,2688]{1,0:T(8,128)} %copy-done.2, f32[8,128]{1,0:T(8,128)} %get-tuple-element.28.refs_3_), custom_call_target="tpu_custom_call" | custom-call | tf_op jit(solution)/shard_map/pallas_call | solution.py:134
  110.6 13.3 %all_to_all.56 = f32[32,1,128]{2,1,0:T(1,128)} all-to-all(f32[32,1,128]{2,1,0:T(1,128)} %bitcast.38), channel_id=1, replica_groups=mesh['tm'=16,'coef'=32] {'coef'}, dimensions={0} | all-to-all | bytes 32768 | tf_op jit(solution)/shard_map/all_to_all | solution.py:144
  123.9 1.9 %shard_map.93 = f32[64,1280]{1,0:T(8,128)} custom-call(s32[1]{0:T(128)} %bitcast.refs_0_, f32[32,128]{1,0:T(8,128)} %bitcast.37, f32[8,1280]{1,0:T(8,128)} %get-tuple-element.34.refs_2_, f32[8,128]{1,0:T(8,128)} %get-tuple-element.28.refs_3_, f32[64,1280]{1,0:T(8,128)} %bitcast.22), custom_call_target="tpu_custom_call" | custom-call | tf_op jit(solution)/shard_map/pallas_call | solution.py:134
  125.7 5.9 %all-to-all-start.4 = ((f32[8,8,1280]{2,1,0:T(8,128)}), f32[8,8,1280]{2,1,0:T(8,128)S(1)}, u32[]{:S(2)}, u32[]{:S(2)}) async-start(f32[8,8,1280]{2,1,0:T(8,128)} %bitcast.26), calls=%async_computation.4 | async-start | bytes 655360 | tf_op jit(solution)/shard_map/all_to_all | solution.py:144
  131.6 2.1 %shard_map.92 = (f32[64,1280]{1,0:T(8,128)}, f32[64,512]{1,0:T(8,128)}) custom-call(f32[8,128]{1,0:T(8,128)} %get-tuple-element.29.refs_0_, f32[64,1280]{1,0:T(8,128)} %bitcast.35, f32[64,1280]{1,0:T(8,128)} %bitcast.23, f32[64,512]{1,0:T(8,128)} %bitcast.31, f32[64,512]{1,0:T(8,128)} %get-tuple-element.30.refs_4_), custom_call_target="tpu_custom_call" | custom-call | tf_op jit(solution)/shard_map/pallas_call | solution.py:134
  133.7 5.1 %all-to-all-done.4 = f32[8,8,1280]{2,1,0:T(8,128)S(1)} async-done(((f32[8,8,1280]{2,1,0:T(8,128)}), f32[8,8,1280]{2,1,0:T(8,128)S(1)}, u32[]{:S(2)}, u32[]{:S(2)}) %all-to-all-start.4) | async-done | bytes 327712 | tf_op jit(solution)/shard_map/all_to_all | solution.py:144
  138.7 0.7 copy.12
  (1 shorter events, 0.0 us)
Async XLA Ops:
  2.5 21.3 %collective-permute-start = (f32[320,256]{1,0:T(8,128)S(1)}, f32[320,256]{1,0:T(8,128)S(1)}, u32[]{:S(2)}, u32[]{:S(2)}) collective-permute-start(f32[320,256]{1,0:T(8,128)S(1)} %pad_maximum_fusion), channel_id=1, source_target_pairs={{32,0},{64,32},{96,64},{128,96},{160,128},{192,160},{224,192},{256... | collective-permute-start | bytes 983048 | tf_op jit(solution)/shard_map/ppermute | solution.py:154
  16.5 18.8 %all-to-all-start = ((f32[32,1,1152]{2,1,0:T(1,128)}), f32[32,1,1152]{2,1,0:T(1,128)S(1)}, u32[]{:S(2)}, u32[]{:S(2)}) async-start(f32[32,1,1152]{2,1,0:T(1,128)} %bitcast.34), calls=%async_computation | async-start | bytes 294912 | tf_op jit(solution)/shard_map/all_to_all | solution.py:144
  23.8 0.7 copy-start.1
  35.3 0.7 copy-start
  37.5 10.1 %collective-permute-start.1 = (f32[8,128]{1,0:T(8,128)}, f32[8,128]{1,0:T(8,128)S(1)}, u32[]{:S(2)}, u32[]{:S(2)}) collective-permute-start(f32[8,128]{1,0:T(8,128)} %get-tuple-element.23.refs_0_), channel_id=1, source_target_pairs={{2,34},{3,35},{6,38},{7,39},{10,42},{11,43},{14,46},{15,47},{18,50... | collective-permute-start | bytes 12296 | tf_op jit(solution)/shard_map/ppermute | solution.py:177
  47.6 0.6 copy-start.3
  97.6 10.6 %collective-permute-start.2 = (f32[8,2688]{1,0:T(8,128)}, f32[8,2688]{1,0:T(8,128)S(1)}, u32[]{:S(2)}, u32[]{:S(2)}) collective-permute-start(f32[8,2688]{1,0:T(8,128)} %shard_map.90.refs_1_), channel_id=1, source_target_pairs={{0,64},{32,96},{64,0},{96,32},{128,192},{160,224},{192,128},{224,1... | collective-permute-start | bytes 258056 | tf_op jit(solution)/shard_map/ppermute | solution.py:189
  108.2 0.6 copy-start.2
  125.7 13.0 %all-to-all-start.4 = ((f32[8,8,1280]{2,1,0:T(8,128)}), f32[8,8,1280]{2,1,0:T(8,128)S(1)}, u32[]{:S(2)}, u32[]{:S(2)}) async-start(f32[8,8,1280]{2,1,0:T(8,128)} %bitcast.26), calls=%async_computation.4 | async-start | bytes 655360 | tf_op jit(solution)/shard_map/all_to_all | solution.py:144

commit v3 on v2

v3 whole, which is shorter than its diff:
```python
import jax
import jax.numpy as jnp
from jax import lax
from jax.experimental import pallas as pl
from jax.experimental.pallas import tpu as pltpu
from jax.sharding import PartitionSpec as P


BLOCK = 256
NN = (((1,), (0,)), ((), ()))
NT = (((1,), (1,)), ((), ()))
F32, BF16 = jnp.float32, jnp.bfloat16


def split(values):
    high = values.astype(BF16)
    return high, (values - high.astype(F32)).astype(BF16)


def times(left, right, dims):
    high, low = split(left)
    count = left.shape[0]
    first = lax.dot_general(jnp.concatenate([high, low], axis=0), right[0], dims, preferred_element_type=F32)
    return first[:count] + first[count:] + lax.dot_general(high, right[1], dims, preferred_element_type=F32)


def skew(rows):
    return pltpu.roll(rows, 0, 1, stride=1, stride_axis=0)


def as_row(column):
    shape = (column.shape[0], 128)
    pick = lax.broadcasted_iota(jnp.int32, shape, 0) == lax.broadcasted_iota(jnp.int32, shape, 1)
    return jnp.sum(jnp.where(pick, jnp.broadcast_to(column, shape), 0.0), axis=0, keepdims=True)


def row_squares(values):
    total = values[:, :128] * values[:, :128]
    for k in range(128, values.shape[1], 128):
        total = total + values[:, k : k + 128] * values[:, k : k + 128]
    return as_row(jnp.sum(total, axis=1, keepdims=True))


def as_column(row, first, count):
    shape = (count, 128)
    pick = lax.broadcasted_iota(jnp.int32, shape, 1) == lax.broadcasted_iota(jnp.int32, shape, 0) + first
    return jnp.sum(jnp.where(pick, jnp.broadcast_to(row[:1], shape), 0.0), axis=1, keepdims=True)


def collect(rows):
    tile, old = rows[:8], rows[8:9]
    for m in range(1, 32):
        tile = tile + rows[9 * m : 9 * m + 8]
        old = old + rows[9 * m + 8 : 9 * m + 9]
    return tile, jnp.broadcast_to(old, (8, 128))


def chunk(tile, rim):
    return jnp.concatenate([tile, rim] * 32, axis=0)


def band(whitening, rim, residual, design):
    taps = jnp.concatenate([whitening, rim[:BLOCK]], axis=0)
    lag = lax.broadcasted_iota(jnp.int32, (BLOCK, BLOCK), 0)
    lane = lax.broadcasted_iota(jnp.int32, (BLOCK, BLOCK), 1)
    mirror = jnp.where((lag + lane) % BLOCK == 0, 1.0, 0.0).astype(BF16)
    high, low = split(taps)
    least = (taps - high.astype(F32) - low.astype(F32)).astype(BF16)
    count = taps.shape[0]
    turned = lax.dot_general(jnp.concatenate([high, low, least], axis=0), mirror, NN, preferred_element_type=F32)
    turned = turned[:count] + turned[count : 2 * count] + turned[2 * count :]
    same, before = [], []
    for b in range(3):
        full = skew(turned[BLOCK * b : BLOCK * (b + 1)])
        same.append(split(jnp.where(lane <= lag, full, 0.0)))
        before.append(split(jnp.where(lane > lag, full, 0.0)))
    res = [residual[:, :BLOCK], residual[:, BLOCK:], rim[BLOCK:]]
    back = [times(res[b], same[b], NN) + times(res[b + 1], before[b + 1], NN) for b in range(2)]
    bands = [jnp.stack([m[k] for m in kind]) for kind in (same, before) for k in range(2)]
    return *bands, times(jnp.concatenate(back, axis=1), split(design()), NN)


def whiten_and_project(gathered, same_high, same_low, before_high, before_low, back_grad, design):
    def block(halves, row):
        return jnp.concatenate(
            [
                jnp.concatenate([gathered[16 * m + row : 16 * m + row + 8] for m in (4 * j + i for i in halves)], axis=1)
                for j in range(8)
            ],
            axis=0,
        )

    same = [(same_high[b], same_low[b]) for b in range(3)]
    before = [(before_high[b], before_low[b]) for b in range(3)]
    plain = [block((2, 3), 8), block((0, 1), 0), block((2, 3), 0), block((0, 1), 8)]
    pred = [times(plain[b + 1], same[b], NT) + times(plain[b], before[b], NT) for b in range(3)]
    own = jnp.concatenate(pred[:2], axis=1)
    energy = jnp.broadcast_to(row_squares(own), (64, 128))
    spread = [times(pred[b], same[b], NN) + times(pred[b + 1], before[b + 1], NN) for b in range(2)]
    grad = times(jnp.concatenate(spread, axis=1), split(design()), NN)
    return jnp.concatenate([back_grad, grad, energy], axis=1), own


def sum_pieces(pieces):
    total = pieces[:8]
    for m in range(1, 8):
        total = total + pieces[8 * m : 8 * m + 8]
    return total


def step_piece(place, mine, other, old):
    total = mine + other
    count = (total.shape[1] - 128) // 2
    alpha = old / total[:, 2 * count :]
    alpha = jnp.where(lax.broadcasted_iota(jnp.int32, alpha.shape, 1) < 64, alpha, 0.0)
    grad = total[:, :count] - as_column(alpha, 8 * place[0], 8) * total[:, count : 2 * count]
    return grad, alpha, jnp.broadcast_to(row_squares(grad), (32, 128))


def direction_piece(place, norms, grad, old, direction):
    norm = jnp.sum(norms, axis=0, keepdims=True)
    beta = as_column(norm, 0, 8) / as_column(old, 8 * place[0], 8)
    mine = direction[pl.ds(pl.multiple_of(8 * place[0], 8), 8), :]
    return jnp.concatenate([grad + beta * mine] * 8, axis=0)


def update(alpha, solution, direction, residual, predicted):
    step = as_column(alpha, 0, 64)
    return solution + step * direction, residual - step * predicted


def run(function, outs, *args, keep=(), close=(), away=()):
    def kernel(*refs):
        values = [r if k in keep else r[...] for k, r in enumerate(refs[: len(args)])]
        results = function(*values)
        results = results if isinstance(results, tuple) else (results,)
        for ref, value in zip(refs[len(args) :], results, strict=True):
            ref[...] = value

    spaces = [pltpu.SMEM if a.dtype == jnp.int32 else pltpu.VMEM for a in args]
    args = [near(a) if k in close else a for k, a in enumerate(args)]
    outs = [s if isinstance(s, tuple) and isinstance(s[0], tuple) else (s, F32) for s in outs]
    got = pl.pallas_call(
        kernel,
        out_shape=[(pltpu.HBM if k in away else pltpu.VMEM)(s, d) for k, (s, d) in enumerate(outs)],
        in_specs=[pl.BlockSpec(memory_space=s) for s in spaces],
        out_specs=[pl.BlockSpec(memory_space=pltpu.VMEM) for _ in outs],
        compiler_params=pltpu.CompilerParams(vmem_limit_bytes=24 << 20),
    )(*args)
    return got if len(outs) > 1 else got[0]


def near(array):
    return pltpu.with_memory_space_constraint(array, pltpu.VMEM)


def far(array):
    return pltpu.with_memory_space_constraint(array, pltpu.HBM)


LIMIT = pltpu.CompilerParams(vmem_limit_bytes=24 << 20)
HBM, VMEM = pl.BlockSpec(memory_space=pltpu.HBM), pl.BlockSpec(memory_space=pltpu.VMEM)


def predict(direction, design, gradient_prev, whitening, residual):
    def kernel(direction, design, gradient_prev, whitening, residual, rows, rim, dir_v, des_v, old_v, rows_v, sems):
        def copy(source, target, k):
            copies.append(pltpu.make_async_copy(source, target, sems.at[k]))
            copies[-1].start()

        copies = []
        copy(direction, dir_v, 0)
        for i in range(4):
            copy(design.at[128 * i : 128 * i + 128], des_v.at[128 * i : 128 * i + 128], 1 + i)
        copy(gradient_prev, old_v, 5)
        copy(whitening.at[:BLOCK], rim.at[:BLOCK], 6)
        copy(residual.at[:, :BLOCK], rim.at[BLOCK:], 7)
        copies[0].wait()
        left = dir_v[...]
        for i in range(4):
            copies[1 + i].wait()
            part = times(left, split(des_v[128 * i : 128 * i + 128]), NT)
            for j in range(8):
                first = 9 * (4 * j + i)
                rows_v[first : first + 8] = part[8 * j : 8 * j + 8]
        copies[5].wait()
        old = row_squares(old_v[...])
        for m in range(32):
            rows_v[9 * m + 8 : 9 * m + 9] = old
        copy(rows_v, rows, 8)
        for k in range(6, 9):
            copies[k].wait()

    return pl.pallas_call(
        kernel,
        out_shape=[
            pltpu.HBM((9 * 32, 128), F32),
            pltpu.HBM((BLOCK + 64, BLOCK), F32),
        ],
        in_specs=[HBM] * 5,
        out_specs=[HBM] * 2,
        scratch_shapes=[
            pltpu.VMEM(direction.shape, F32),
            pltpu.VMEM(design.shape, F32),
            pltpu.VMEM(gradient_prev.shape, F32),
            pltpu.VMEM((9 * 32, 128), F32),
            pltpu.SemaphoreType.DMA((9,)),
        ],
        compiler_params=LIMIT,
        name="predict",
    )(*[far(a) for a in (direction, design, gradient_prev, whitening, residual)])


def banded(whitening, rim, residual, design):
    def kernel(rim, whitening, residual, design, b0, b1, b2, b3, back_grad, tap_v, res_v, des_v, sems):
        copies = [
            pltpu.make_async_copy(source, target, sems.at[k])
            for k, (source, target) in enumerate(((whitening, tap_v), (residual, res_v), (design, des_v)))
        ]
        for copy in copies:
            copy.start()
        for copy in copies[:2]:
            copy.wait()

        def fetched():
            copies[2].wait()
            return des_v[...]

        b0[...], b1[...], b2[...], b3[...], back_grad[...] = band(tap_v[...], rim[...], res_v[...], fetched)

    args = (whitening, residual, design)
    return pl.pallas_call(
        kernel,
        out_shape=[pltpu.VMEM((3, BLOCK, BLOCK), BF16)] * 4 + [pltpu.VMEM((64, design.shape[1]), F32)],
        in_specs=[VMEM] + [HBM] * 3,
        out_specs=[VMEM] * 5,
        scratch_shapes=[pltpu.VMEM(a.shape, F32) for a in args] + [pltpu.SemaphoreType.DMA((3,))],
        compiler_params=LIMIT,
        name="band",
    )(near(rim), *[far(a) for a in args])


def project(gathered, bands, back_grad, design):
    def kernel(gathered, b0, b1, b2, b3, back_grad, design, pieces, predicted, des_v, sem):
        copy = pltpu.make_async_copy(design, des_v, sem)
        copy.start()

        def fetched():
            copy.wait()
            return des_v[...]

        pieces[...], predicted[...] = whiten_and_project(
            gathered[...], b0[...], b1[...], b2[...], b3[...], back_grad[...], fetched
        )

    return pl.pallas_call(
        kernel,
        out_shape=[pltpu.VMEM((64, 2 * design.shape[1] + 128), F32), pltpu.VMEM((64, design.shape[0]), F32)],
        in_specs=[VMEM] * 6 + [HBM],
        out_specs=[VMEM] * 2,
        scratch_shapes=[pltpu.VMEM(design.shape, F32), pltpu.SemaphoreType.DMA],
        compiler_params=LIMIT,
        name="whiten_and_project",
    )(near(gathered), *[near(b) for b in bands], near(back_grad), far(design))


def exchange(rows, axis, groups=None):
    return lax.all_to_all(rows, axis, 0, 0, axis_index_groups=groups, tiled=True)


def per_device(design, whitening, solution, direction, gradient_prev, residual):
    blocks_t, blocks_c = lax.axis_size("tm"), lax.axis_size("coef")
    coefs = design.shape[1]
    solution, direction, gradient_prev, residual = solution.T, direction.T, gradient_prev.T, residual.T
    groups = [[4 * x + 2 * z + k for x in range(4) for k in range(2)] for z in range(2)]
    t = lax.axis_index("tm").astype(jnp.int32)
    place = (lax.shift_right_logical(t, 2) * 2 + (t & 1))[None]
    rows, rim = predict(direction, design, gradient_prev, whitening, residual)
    rows = exchange(rows.reshape(32, 9 * 128), "coef").reshape(9 * 32, 128)
    rim = lax.ppermute(rim, "tm", [(i + 1, i) for i in range(blocks_t - 1)])
    tile, old = run(collect, [(8, 128), (8, 128)], rows, close=(0,))
    pairs = []
    for t in range(blocks_t):
        for c in range(blocks_c):
            to = t + 1 if c % 4 >= 2 else t - 1
            if 0 <= to < blocks_t:
                pairs.append((t * blocks_c + c, to * blocks_c + c))
    rim_tile = lax.ppermute(tile, ("tm", "coef"), pairs)
    gathered = exchange(run(chunk, [(16 * 32, 128)], tile, rim_tile, close=(0, 1), away=(0,)), "coef")
    *bands, back_grad = banded(whitening, rim, residual, design)
    pieces, predicted = project(gathered, bands, back_grad, design)
    mine = run(sum_pieces, [(8, 2 * coefs + 128)], exchange(pieces, "tm", groups), close=(0,))
    other = lax.ppermute(mine, "tm", [(i, i ^ 2) for i in range(blocks_t)])
    grad, alpha, norms = run(
        step_piece, [(8, coefs), (8, 128), (32, 128)], place, mine, other, old, keep=(0,), close=(1, 2, 3)
    )
    norms = exchange(norms, "coef")
    new_solution, new_residual = run(
        update,
        [solution.shape, residual.shape],
        alpha,
        solution,
        direction,
        residual,
        predicted,
        close=(0, 4),
        away=(0, 1),
    )
    pieces = run(direction_piece, [(64, coefs)], place, norms, grad, old, direction, keep=(0, 4), close=(1, 2, 3), away=(0,))
    return new_solution.T, new_residual.T, exchange(pieces, "tm", groups).T


def solution(mesh):
    return jax.shard_map(
        per_device,
        mesh=mesh,
        in_specs=(
            P("tm", "coef"),
            P("tm", None),
            P("coef", None),
            P("coef", None),
            P("coef", None),
            P("tm", None),
        ),
        out_specs=(P("coef", None), P("tm", None), P("coef", None)),
        check_vma=False,
    )
```

time: 140 us -> 136 us (0.971)
  Pallas kernels: 28.8 us -> 20 us
  waiting for transfers between devices: 24.7 us -> 32.7 us
  blocking collectives: 52.7 us -> 60.3 us
  starting transfers between devices: 27.3 us -> 20.6 us
  local copies, waits for them, and re-layouts: 5.15 us -> 0.74 us
    ppermute x1, waiting for transfers between devices: 0.01 us -> 14.1 us  [per_device(): rim = lax.ppermute(rim, 'tm', [(i + 1, i) for i in range(blocks_t - 1)])]
    pallas_call x9, Pallas kernels: 28.8 us -> 20 us  [the longest x1 11.1 us: predict(): pl.pallas_call(kernel, out_shape=[pltpu.HBM((9 * 32, 128), F32), pltpu.HB...]
    all_to_all x3, blocking collectives: 52.7 us -> 60.3 us  [exchange(): lax.all_to_all(rows, axis, 0, 0, axis_index_groups=groups, tiled=True)]
    ppermute x1, starting transfers between devices: 8.75 us -> 1.92 us  [per_device(): rim = lax.ppermute(rim, 'tm', [(i + 1, i) for i in range(blocks_t - 1)])]
    all_to_all x2, waiting for transfers between devices: 9.42 us -> 6.22 us  [exchange(): lax.all_to_all(rows, axis, 0, 0, axis_index_groups=groups, tiled=True)]
    unnamed x9 -> x7, local copies, waits for them, and re-layouts: 3.33 us -> 0.74 us
    all_to_all x2, starting transfers between devices: 13.2 us -> 10.7 us  [exchange(): lax.all_to_all(rows, axis, 0, 0, axis_index_groups=groups, tiled=True)]
    ppermute x1, waiting for transfers between devices: 7.58 us -> 5.28 us  [per_device(): other = lax.ppermute(mine, 'tm', [(i, i ^ 2) for i in range(blocks_t)])]
  transfers between devices with their start and end apart: 5 -> 5, of which waited for: 4 -> 4; matrix products, arithmetic and copies ran while one was open for 0% -> 0% of each run, Pallas kernels for 10% -> 3%
where the time goes in v3:
time: 136 us; the launch traced here: 135 us
  blocking collectives  60.3 us (44%)
  waiting for transfers between devices  32.7 us (24%)
  starting transfers between devices  20.6 us (15%)
  Pallas kernels  20 us (15%)
    all_to_all x3, blocking collectives, exchange(): lax.all_to_all(rows, axis, 0, 0, axis_index_groups=groups, tiled=True)  60.3 us
    ppermute x1, waiting for transfers between devices, per_device(): rim = lax.ppermute(rim, 'tm', [(i + 1, i) for i in range(blocks_t - 1)])  14.1 us
    pallas_call x1, Pallas kernels, predict(): pl.pallas_call(kernel, out_shape=[pltpu.HBM((9 * 32, 128), F32), pltpu.HB...  11.1 us
    all_to_all x2, starting transfers between devices, exchange(): lax.all_to_all(rows, axis, 0, 0, axis_index_groups=groups, tiled=True)  10.7 us
    ppermute x1, waiting for transfers between devices, per_device(): rim_tile = lax.ppermute(tile, ('tm', 'coef'), pairs)  7.19 us
    all_to_all x2, waiting for transfers between devices, exchange(): lax.all_to_all(rows, axis, 0, 0, axis_index_groups=groups, tiled=True)  6.22 us
    ppermute x1, waiting for transfers between devices, per_device(): other = lax.ppermute(mine, 'tm', [(i, i ^ 2) for i in range(blocks_t)])  5.28 us
    ppermute x1, starting transfers between devices, per_device(): rim_tile = lax.ppermute(tile, ('tm', 'coef'), pairs)  4.18 us
  transfers between devices with their start and end apart: 5, of which 4 were waited for; matrix products, arithmetic and copies ran while one was open for 0% of the time, Pallas kernels for 3%

profile of v3, /device:TPU:1, one launch (start us, length us, event | category | flops | bytes accessed | tf_op | source)
XLA Modules:
  0.0 135.2 jit_solution(8871217827994103123)
XLA Ops:
  0.6 11.1 %predict.1 = (f32[288,128]{1,0:T(8,128)}, f32[320,256]{1,0:T(8,128)}) custom-call(f32[64,1280]{1,0:T(8,128)} %bitcast.21, f32[512,1280]{1,0:T(8,128)} %design.5, f32[64,1280]{1,0:T(8,128)} %bitcast.37, f32[512,256]{1,0:T(8,128)} %whitening.3, f32[64,512]{1,0:T(8,128)} %bitcast.25), custom_call_target="tpu_custom_call" | custom-call | tf_op jit(solution)/shard_map/predict/pallas_call | solution.py:194
  11.8 23.5 %all_to_all.54 = f32[32,1,1152]{2,1,0:T(1,128)S(1)} all-to-all(f32[32,1,1152]{2,1,0:T(1,128)} %bitcast.38), channel_id=1, replica_groups=mesh['tm'=16,'coef'=32] {'coef'}, dimensions={0} | all-to-all | bytes 294912 | tf_op jit(solution)/shard_map/all_to_all | solution.py:268
  35.3 4.2 %collective-permute-start = (f32[8,128]{1,0:T(8,128)S(1)}, f32[8,128]{1,0:T(8,128)S(1)}, u32[]{:S(2)}, u32[]{:S(2)}) collective-permute-start(f32[8,128]{1,0:T(8,128)S(1)} %get-tuple-element.20.refs_0_), channel_id=1, source_target_pairs={{2,34},{3,35},{6,38},{7,39},{10,42},{11,43},{14,46},{15,47},{18,50... | collective-permute-start | bytes 12296 | tf_op jit(solution)/shard_map/ppermute | solution.py:288
  39.5 7.2 %collective-permute-done.refs_1_ = f32[8,128]{1,0:T(8,128)S(1)} collective-permute-done((f32[8,128]{1,0:T(8,128)S(1)}, f32[8,128]{1,0:T(8,128)S(1)}, u32[]{:S(2)}, u32[]{:S(2)}) %collective-permute-start) | collective-permute-done | bytes 4128 | tf_op jit(solution)/shard_map/ppermute | solution.py:288
  46.7 0.7 shard_map.86
  47.4 3.9 %all-to-all-start.1 = ((f32[32,16,128]{2,1,0:T(8,128)}), f32[32,16,128]{2,1,0:T(8,128)S(1)}, u32[]{:S(2)}, u32[]{:S(2)}) async-start(f32[32,16,128]{2,1,0:T(8,128)} %bitcast.36), calls=%async_computation.1 | async-start | bytes 524288 | tf_op jit(solution)/shard_map/all_to_all | solution.py:268
  51.3 1.9 %collective-permute-start.1 = (f32[320,256]{1,0:T(8,128)}, f32[320,256]{1,0:T(8,128)S(1)}, u32[]{:S(2)}, u32[]{:S(2)}) collective-permute-start(f32[320,256]{1,0:T(8,128)} %get-tuple-element.21), channel_id=1, source_target_pairs={{32,0},{64,32},{96,64},{128,96},{160,128},{192,160},{224,192},{256... | collective-permute-start | bytes 983048 | tf_op jit(solution)/shard_map/ppermute | solution.py:280
  53.2 14.1 %collective-permute-done.1.rim = f32[320,256]{1,0:T(8,128)S(1)} collective-permute-done((f32[320,256]{1,0:T(8,128)}, f32[320,256]{1,0:T(8,128)S(1)}, u32[]{:S(2)}, u32[]{:S(2)}) %collective-permute-start.1) | collective-permute-done | bytes 327712 | tf_op jit(solution)/shard_map/ppermute | solution.py:280
  67.3 3.1 %band.1 = (bf16[3,256,256]{2,1,0:T(8,128)(2,1)S(1)}, bf16[3,256,256]{2,1,0:T(8,128)(2,1)S(1)}, bf16[3,256,256]{2,1,0:T(8,128)(2,1)S(1)}, bf16[3,256,256]{2,1,0:T(8,128)(2,1)S(1)}, f32[64,1280]{1,0:T(8,128)S(1)}) custom-call(f32[320,256]{1,0:T(8,128)S(1)} %collective-permute-done.1.rim, f32[512,256]{1,0:T(8,128)} %whitening.3, f32[64,512]{1,0:T(8,128)} %bitcast.26, ...), custom_call_target="tpu_custom_call" | custom-call | tf_op jit(solution)/shard_map/band/pallas_call | solution.py:232
  70.4 0.0 all-to-all-done.1
  70.4 0.0 copy-start
  70.4 3.0 %whiten_and_project.1 = (f32[64,2688]{1,0:T(8,128)S(1)}, f32[64,512]{1,0:T(8,128)S(1)}) custom-call(f32[512,128]{1,0:T(8,128)S(1)} %bitcast.28, bf16[3,256,256]{2,1,0:T(8,128)(2,1)S(1)} %get-tuple-element.22.b0, bf16[3,256,256]{2,1,0:T(8,128)(2,1)S(1)} %get-tuple-element.23.b1, bf16[3,256,256]{2,1,0:T(8,128)(2,1)S(1)} %get-tuple-element.24.b2, ...), custom_call_target="tpu_custom_call" | custom-call | tf_op jit(solution)/shard_map/whiten_and_project/pallas_call | solution.py:256
  73.5 0.0 copy-start.1
  73.5 0.0 copy-start.2
  73.5 16.2 %all_to_all.55 = f32[8,8,2688]{2,1,0:T(8,128)S(1)} all-to-all(f32[8,8,2688]{2,1,0:T(8,128)S(1)} %bitcast.29), channel_id=1, replica_groups={{0,32,128,160,256,288,384,416},{64,96,192,224,320,352,448,480},{1,33,12..., dimensions={0} | all-to-all | bytes 1376256 | tf_op jit(solution)/shard_map/all_to_all | solution.py:268
  89.8 3.8 %collective-permute-start.2 = (f32[8,2688]{1,0:T(8,128)S(1)}, f32[8,2688]{1,0:T(8,128)S(1)}, u32[]{:S(2)}, u32[]{:S(2)}) collective-permute-start(f32[8,2688]{1,0:T(8,128)S(1)} %shard_map.87.refs_1_), channel_id=1, source_target_pairs={{0,64},{32,96},{64,0},{96,32},{128,192},{160,224},{192,128},{224,1... | collective-permute-start | bytes 258056 | tf_op jit(solution)/shard_map/ppermute | solution.py:293
  93.7 5.3 %collective-permute-done.2.refs_2_ = f32[8,2688]{1,0:T(8,128)S(1)} collective-permute-done((f32[8,2688]{1,0:T(8,128)S(1)}, f32[8,2688]{1,0:T(8,128)S(1)}, u32[]{:S(2)}, u32[]{:S(2)}) %collective-permute-start.2) | collective-permute-done | bytes 86048 | tf_op jit(solution)/shard_map/ppermute | solution.py:293
  98.9 0.2 shard_map.88
  99.1 20.6 %all_to_all.56 = f32[32,1,128]{2,1,0:T(1,128)S(1)} all-to-all(f32[32,1,128]{2,1,0:T(1,128)S(1)} %bitcast.33), channel_id=1, replica_groups=mesh['tm'=16,'coef'=32] {'coef'}, dimensions={0} | all-to-all | bytes 32768 | tf_op jit(solution)/shard_map/all_to_all | solution.py:268
  119.7 0.0 copy-done
  119.7 0.8 shard_map.90
  120.5 6.8 %all-to-all-start.4 = ((f32[8,8,1280]{2,1,0:T(8,128)}), f32[8,8,1280]{2,1,0:T(8,128)S(1)}, u32[]{:S(2)}, u32[]{:S(2)}) async-start(f32[8,8,1280]{2,1,0:T(8,128)} %bitcast.35), calls=%async_computation.4 | async-start | bytes 655360 | tf_op jit(solution)/shard_map/all_to_all | solution.py:268
  127.3 0.0 copy-done.1
  127.3 0.0 copy-done.2
  127.3 0.9 shard_map.89
  128.2 6.2 %all-to-all-done.4 = f32[8,8,1280]{2,1,0:T(8,128)S(1)} async-done(((f32[8,8,1280]{2,1,0:T(8,128)}), f32[8,8,1280]{2,1,0:T(8,128)S(1)}, u32[]{:S(2)}, u32[]{:S(2)}) %all-to-all-start.4) | async-done | bytes 327712 | tf_op jit(solution)/shard_map/all_to_all | solution.py:268
  134.4 0.7 copy.12
  (2 shorter events, 0.1 us)
Async XLA Ops:
  35.3 11.4 %collective-permute-start = (f32[8,128]{1,0:T(8,128)S(1)}, f32[8,128]{1,0:T(8,128)S(1)}, u32[]{:S(2)}, u32[]{:S(2)}) collective-permute-start(f32[8,128]{1,0:T(8,128)S(1)} %get-tuple-element.20.refs_0_), channel_id=1, source_target_pairs={{2,34},{3,35},{6,38},{7,39},{10,42},{11,43},{14,46},{15,47},{18,50... | collective-permute-start | bytes 12296 | tf_op jit(solution)/shard_map/ppermute | solution.py:288
  47.4 23.0 %all-to-all-start.1 = ((f32[32,16,128]{2,1,0:T(8,128)}), f32[32,16,128]{2,1,0:T(8,128)S(1)}, u32[]{:S(2)}, u32[]{:S(2)}) async-start(f32[32,16,128]{2,1,0:T(8,128)} %bitcast.36), calls=%async_computation.1 | async-start | bytes 524288 | tf_op jit(solution)/shard_map/all_to_all | solution.py:268
  51.3 16.0 %collective-permute-start.1 = (f32[320,256]{1,0:T(8,128)}, f32[320,256]{1,0:T(8,128)S(1)}, u32[]{:S(2)}, u32[]{:S(2)}) collective-permute-start(f32[320,256]{1,0:T(8,128)} %get-tuple-element.21), channel_id=1, source_target_pairs={{32,0},{64,32},{96,64},{128,96},{160,128},{192,160},{224,192},{256... | collective-permute-start | bytes 983048 | tf_op jit(solution)/shard_map/ppermute | solution.py:280
  70.4 49.3 %copy-start = (f32[1280,64]{0,1:T(8,128)S(1)}, f32[1280,64]{0,1:T(8,128)}, u32[]{:S(2)}) copy-start(f32[1280,64]{0,1:T(8,128)} %param.9) | copy-start | bytes 983044
  73.5 53.9 %copy-start.1 = (f32[512,64]{0,1:T(8,128)S(1)}, f32[512,64]{0,1:T(8,128)}, u32[]{:S(2)}) copy-start(f32[512,64]{0,1:T(8,128)} %param.11) | copy-start | bytes 393220
  73.5 53.8 %copy-start.2 = (f32[1280,64]{0,1:T(8,128)S(1)}, f32[1280,64]{0,1:T(8,128)}, u32[]{:S(2)}) copy-start(f32[1280,64]{0,1:T(8,128)} %param.8) | copy-start | bytes 983044
  89.8 9.1 %collective-permute-start.2 = (f32[8,2688]{1,0:T(8,128)S(1)}, f32[8,2688]{1,0:T(8,128)S(1)}, u32[]{:S(2)}, u32[]{:S(2)}) collective-permute-start(f32[8,2688]{1,0:T(8,128)S(1)} %shard_map.87.refs_1_), channel_id=1, source_target_pairs={{0,64},{32,96},{64,0},{96,32},{128,192},{160,224},{192,128},{224,1... | collective-permute-start | bytes 258056 | tf_op jit(solution)/shard_map/ppermute | solution.py:293
  120.5 13.9 %all-to-all-start.4 = ((f32[8,8,1280]{2,1,0:T(8,128)}), f32[8,8,1280]{2,1,0:T(8,128)S(1)}, u32[]{:S(2)}, u32[]{:S(2)}) async-start(f32[8,8,1280]{2,1,0:T(8,128)} %bitcast.35), calls=%async_computation.4 | async-start | bytes 655360 | tf_op jit(solution)/shard_map/all_to_all | solution.py:268

commit v4 on v3

--- a/solution.py
+++ b/solution.py
@@ -195,10 +195,10 @@
         kernel,
         out_shape=[
             pltpu.HBM((9 * 32, 128), F32),
-            pltpu.HBM((BLOCK + 64, BLOCK), F32),
+            pltpu.VMEM((BLOCK + 64, BLOCK), F32),
         ],
         in_specs=[HBM] * 5,
-        out_specs=[HBM] * 2,
+        out_specs=[HBM, VMEM],
         scratch_shapes=[
             pltpu.VMEM(direction.shape, F32),
             pltpu.VMEM(design.shape, F32),
@@ -278,6 +278,7 @@
     rows, rim = predict(direction, design, gradient_prev, whitening, residual)
     rows = exchange(rows.reshape(32, 9 * 128), "coef").reshape(9 * 32, 128)
     rim = lax.ppermute(rim, "tm", [(i + 1, i) for i in range(blocks_t - 1)])
+    *bands, back_grad = banded(whitening, rim, residual, design)
     tile, old = run(collect, [(8, 128), (8, 128)], rows, close=(0,))
     pairs = []
     for t in range(blocks_t):
@@ -286,8 +287,7 @@
             if 0 <= to < blocks_t:
                 pairs.append((t * blocks_c + c, to * blocks_c + c))
     rim_tile = lax.ppermute(tile, ("tm", "coef"), pairs)
-    gathered = exchange(run(chunk, [(16 * 32, 128)], tile, rim_tile, close=(0, 1), away=(0,)), "coef")
-    *bands, back_grad = banded(whitening, rim, residual, design)
+    gathered = exchange(run(chunk, [(16 * 32, 128)], tile, rim_tile, close=(0, 1)), "coef")
     pieces, predicted = project(gathered, bands, back_grad, design)
     mine = run(sum_pieces, [(8, 2 * coefs + 128)], exchange(pieces, "tm", groups), close=(0,))
     other = lax.ppermute(mine, "tm", [(i, i ^ 2) for i in range(blocks_t)])

time: 136 us -> 128 us (0.941)
  Pallas kernels: 20 us -> 12.8 us
    pallas_call x1, Pallas kernels: 11.1 us -> 3.96 us  [predict(): pl.pallas_call(kernel, out_shape=[pltpu.HBM((9 * 32, 128), F32), pltpu.VM...]
where the time goes in v4:
time: 128 us; the launch traced here: 127 us
  blocking collectives  60.1 us (47%)
  waiting for transfers between devices  32.9 us (26%)
  starting transfers between devices  19.7 us (15%)
  Pallas kernels  12.8 us (10%)
    all_to_all x3, blocking collectives, exchange(): lax.all_to_all(rows, axis, 0, 0, axis_index_groups=groups, tiled=True)  60.1 us
    ppermute x1, waiting for transfers between devices, per_device(): rim = lax.ppermute(rim, 'tm', [(i + 1, i) for i in range(blocks_t - 1)])  14 us
    all_to_all x2, starting transfers between devices, exchange(): lax.all_to_all(rows, axis, 0, 0, axis_index_groups=groups, tiled=True)  9.97 us
    ppermute x1, waiting for transfers between devices, per_device(): rim_tile = lax.ppermute(tile, ('tm', 'coef'), pairs)  7.19 us
    all_to_all x2, waiting for transfers between devices, exchange(): lax.all_to_all(rows, axis, 0, 0, axis_index_groups=groups, tiled=True)  6.22 us
    ppermute x1, waiting for transfers between devices, per_device(): other = lax.ppermute(mine, 'tm', [(i, i ^ 2) for i in range(blocks_t)])  5.49 us
    ppermute x1, starting transfers between devices, per_device(): rim_tile = lax.ppermute(tile, ('tm', 'coef'), pairs)  4.18 us
    pallas_call x1, Pallas kernels, predict(): pl.pallas_call(kernel, out_shape=[pltpu.HBM((9 * 32, 128), F32), pltpu.VM...  3.96 us
  transfers between devices with their start and end apart: 5, of which 4 were waited for; matrix products, arithmetic and copies ran while one was open for 0% of the time, Pallas kernels for 3%

profile of v4, /device:TPU:1, one launch (start us, length us, event | category | flops | bytes accessed | tf_op | source)
XLA Modules:
  0.0 127.1 jit_solution(3378523955850598294)
XLA Ops:
  0.6 4.0 %predict.1 = (f32[288,128]{1,0:T(8,128)}, f32[320,256]{1,0:T(8,128)S(1)}) custom-call(f32[64,1280]{1,0:T(8,128)} %bitcast.21, f32[512,1280]{1,0:T(8,128)} %design.5, f32[64,1280]{1,0:T(8,128)} %bitcast.36, f32[512,256]{1,0:T(8,128)} %whitening.3, f32[64,512]{1,0:T(8,128)} %bitcast.25), custom_call_target="tpu_custom_call" | custom-call | tf_op jit(solution)/shard_map/predict/pallas_call | solution.py:194
  4.6 23.5 %all_to_all.54 = f32[32,1,1152]{2,1,0:T(1,128)S(1)} all-to-all(f32[32,1,1152]{2,1,0:T(1,128)} %bitcast.37), channel_id=1, replica_groups=mesh['tm'=16,'coef'=32] {'coef'}, dimensions={0} | all-to-all | bytes 294912 | tf_op jit(solution)/shard_map/all_to_all | solution.py:268
  28.2 4.2 %collective-permute-start = (f32[8,128]{1,0:T(8,128)S(1)}, f32[8,128]{1,0:T(8,128)S(1)}, u32[]{:S(2)}, u32[]{:S(2)}) collective-permute-start(f32[8,128]{1,0:T(8,128)S(1)} %get-tuple-element.20.refs_0_), channel_id=1, source_target_pairs={{2,34},{3,35},{6,38},{7,39},{10,42},{11,43},{14,46},{15,47},{18,50... | collective-permute-start | bytes 12296 | tf_op jit(solution)/shard_map/ppermute | solution.py:289
  32.4 7.2 %collective-permute-done.refs_1_ = f32[8,128]{1,0:T(8,128)S(1)} collective-permute-done((f32[8,128]{1,0:T(8,128)S(1)}, f32[8,128]{1,0:T(8,128)S(1)}, u32[]{:S(2)}, u32[]{:S(2)}) %collective-permute-start) | collective-permute-done | bytes 4128 | tf_op jit(solution)/shard_map/ppermute | solution.py:289
  39.5 0.7 shard_map.86
  40.3 3.9 %all-to-all-start.1 = ((f32[32,16,128]{2,1,0:T(8,128)}), f32[32,16,128]{2,1,0:T(8,128)S(1)}, u32[]{:S(2)}, u32[]{:S(2)}) async-start(f32[32,16,128]{2,1,0:T(8,128)} %bitcast.6), calls=%async_computation.1 | async-start | bytes 524288 | tf_op jit(solution)/shard_map/all_to_all | solution.py:268
  44.1 1.9 %collective-permute-start.1 = (f32[320,256]{1,0:T(8,128)S(1)}, f32[320,256]{1,0:T(8,128)S(1)}, u32[]{:S(2)}, u32[]{:S(2)}) collective-permute-start(f32[320,256]{1,0:T(8,128)S(1)} %get-tuple-element.21), channel_id=1, source_target_pairs={{32,0},{64,32},{96,64},{128,96},{160,128},{192,160},{224,192},{256... | collective-permute-start | bytes 983048 | tf_op jit(solution)/shard_map/ppermute | solution.py:280
  46.1 14.0 %collective-permute-done.1.rim = f32[320,256]{1,0:T(8,128)S(1)} collective-permute-done((f32[320,256]{1,0:T(8,128)S(1)}, f32[320,256]{1,0:T(8,128)S(1)}, u32[]{:S(2)}, u32[]{:S(2)}) %collective-permute-start.1) | collective-permute-done | bytes 327712 | tf_op jit(solution)/shard_map/ppermute | solution.py:280
  60.1 3.1 %band.1 = (bf16[3,256,256]{2,1,0:T(8,128)(2,1)S(1)}, bf16[3,256,256]{2,1,0:T(8,128)(2,1)S(1)}, bf16[3,256,256]{2,1,0:T(8,128)(2,1)S(1)}, bf16[3,256,256]{2,1,0:T(8,128)(2,1)S(1)}, f32[64,1280]{1,0:T(8,128)S(1)}) custom-call(f32[320,256]{1,0:T(8,128)S(1)} %collective-permute-done.1.rim, f32[512,256]{1,0:T(8,128)} %whitening.3, f32[64,512]{1,0:T(8,128)} %bitcast.26, ...), custom_call_target="tpu_custom_call" | custom-call | tf_op jit(solution)/shard_map/band/pallas_call | solution.py:232
  63.3 0.0 all-to-all-done.1
  63.3 0.0 copy-start
  63.3 3.0 %whiten_and_project.1 = (f32[64,2688]{1,0:T(8,128)S(1)}, f32[64,512]{1,0:T(8,128)S(1)}) custom-call(f32[512,128]{1,0:T(8,128)S(1)} %bitcast.28, bf16[3,256,256]{2,1,0:T(8,128)(2,1)S(1)} %get-tuple-element.22.b0, bf16[3,256,256]{2,1,0:T(8,128)(2,1)S(1)} %get-tuple-element.23.b1, bf16[3,256,256]{2,1,0:T(8,128)(2,1)S(1)} %get-tuple-element.24.b2, ...), custom_call_target="tpu_custom_call" | custom-call | tf_op jit(solution)/shard_map/whiten_and_project/pallas_call | solution.py:256
  66.3 0.0 copy-start.1
  66.3 0.0 copy-start.2
  66.4 16.3 %all_to_all.55 = f32[8,8,2688]{2,1,0:T(8,128)S(1)} all-to-all(f32[8,8,2688]{2,1,0:T(8,128)S(1)} %bitcast.29), channel_id=1, replica_groups={{0,32,128,160,256,288,384,416},{64,96,192,224,320,352,448,480},{1,33,12..., dimensions={0} | all-to-all | bytes 1376256 | tf_op jit(solution)/shard_map/all_to_all | solution.py:268
  82.7 3.6 %collective-permute-start.2 = (f32[8,2688]{1,0:T(8,128)S(1)}, f32[8,2688]{1,0:T(8,128)S(1)}, u32[]{:S(2)}, u32[]{:S(2)}) collective-permute-start(f32[8,2688]{1,0:T(8,128)S(1)} %shard_map.87.refs_1_), channel_id=1, source_target_pairs={{0,64},{32,96},{64,0},{96,32},{128,192},{160,224},{192,128},{224,1... | collective-permute-start | bytes 258056 | tf_op jit(solution)/shard_map/ppermute | solution.py:293
  86.4 5.5 %collective-permute-done.2.refs_2_ = f32[8,2688]{1,0:T(8,128)S(1)} collective-permute-done((f32[8,2688]{1,0:T(8,128)S(1)}, f32[8,2688]{1,0:T(8,128)S(1)}, u32[]{:S(2)}, u32[]{:S(2)}) %collective-permute-start.2) | collective-permute-done | bytes 86048 | tf_op jit(solution)/shard_map/ppermute | solution.py:293
  91.9 0.2 shard_map.88
  92.0 20.3 %all_to_all.56 = f32[32,1,128]{2,1,0:T(1,128)S(1)} all-to-all(f32[32,1,128]{2,1,0:T(1,128)S(1)} %bitcast.33), channel_id=1, replica_groups=mesh['tm'=16,'coef'=32] {'coef'}, dimensions={0} | all-to-all | bytes 32768 | tf_op jit(solution)/shard_map/all_to_all | solution.py:268
  112.3 0.0 copy-done
  112.3 0.8 shard_map.90
  113.2 6.1 %all-to-all-start.4 = ((f32[8,8,1280]{2,1,0:T(8,128)}), f32[8,8,1280]{2,1,0:T(8,128)S(1)}, u32[]{:S(2)}, u32[]{:S(2)}) async-start(f32[8,8,1280]{2,1,0:T(8,128)} %bitcast.35), calls=%async_computation.4 | async-start | bytes 655360 | tf_op jit(solution)/shard_map/all_to_all | solution.py:268
  119.3 0.0 copy-done.1
  119.3 0.0 copy-done.2
  119.3 0.9 shard_map.89
  120.2 6.2 %all-to-all-done.4 = f32[8,8,1280]{2,1,0:T(8,128)S(1)} async-done(((f32[8,8,1280]{2,1,0:T(8,128)}), f32[8,8,1280]{2,1,0:T(8,128)S(1)}, u32[]{:S(2)}, u32[]{:S(2)}) %all-to-all-start.4) | async-done | bytes 327712 | tf_op jit(solution)/shard_map/all_to_all | solution.py:268
  126.4 0.7 copy.12
  (2 shorter events, 0.1 us)
Async XLA Ops:
  28.2 11.4 %collective-permute-start = (f32[8,128]{1,0:T(8,128)S(1)}, f32[8,128]{1,0:T(8,128)S(1)}, u32[]{:S(2)}, u32[]{:S(2)}) collective-permute-start(f32[8,128]{1,0:T(8,128)S(1)} %get-tuple-element.20.refs_0_), channel_id=1, source_target_pairs={{2,34},{3,35},{6,38},{7,39},{10,42},{11,43},{14,46},{15,47},{18,50... | collective-permute-start | bytes 12296 | tf_op jit(solution)/shard_map/ppermute | solution.py:289
  40.3 23.0 %all-to-all-start.1 = ((f32[32,16,128]{2,1,0:T(8,128)}), f32[32,16,128]{2,1,0:T(8,128)S(1)}, u32[]{:S(2)}, u32[]{:S(2)}) async-start(f32[32,16,128]{2,1,0:T(8,128)} %bitcast.6), calls=%async_computation.1 | async-start | bytes 524288 | tf_op jit(solution)/shard_map/all_to_all | solution.py:268
  44.1 16.0 %collective-permute-start.1 = (f32[320,256]{1,0:T(8,128)S(1)}, f32[320,256]{1,0:T(8,128)S(1)}, u32[]{:S(2)}, u32[]{:S(2)}) collective-permute-start(f32[320,256]{1,0:T(8,128)S(1)} %get-tuple-element.21), channel_id=1, source_target_pairs={{32,0},{64,32},{96,64},{128,96},{160,128},{192,160},{224,192},{256... | collective-permute-start | bytes 983048 | tf_op jit(solution)/shard_map/ppermute | solution.py:280
  63.3 49.1 %copy-start = (f32[1280,64]{0,1:T(8,128)S(1)}, f32[1280,64]{0,1:T(8,128)}, u32[]{:S(2)}) copy-start(f32[1280,64]{0,1:T(8,128)} %param.9) | copy-start | bytes 983044
  66.3 52.9 %copy-start.1 = (f32[512,64]{0,1:T(8,128)S(1)}, f32[512,64]{0,1:T(8,128)}, u32[]{:S(2)}) copy-start(f32[512,64]{0,1:T(8,128)} %param.11) | copy-start | bytes 393220
  66.3 52.9 %copy-start.2 = (f32[1280,64]{0,1:T(8,128)S(1)}, f32[1280,64]{0,1:T(8,128)}, u32[]{:S(2)}) copy-start(f32[1280,64]{0,1:T(8,128)} %param.8) | copy-start | bytes 983044
  82.7 9.1 %collective-permute-start.2 = (f32[8,2688]{1,0:T(8,128)S(1)}, f32[8,2688]{1,0:T(8,128)S(1)}, u32[]{:S(2)}, u32[]{:S(2)}) collective-permute-start(f32[8,2688]{1,0:T(8,128)S(1)} %shard_map.87.refs_1_), channel_id=1, source_target_pairs={{0,64},{32,96},{64,0},{96,32},{128,192},{160,224},{192,128},{224,1... | collective-permute-start | bytes 258056 | tf_op jit(solution)/shard_map/ppermute | solution.py:293
  113.2 13.2 %all-to-all-start.4 = ((f32[8,8,1280]{2,1,0:T(8,128)}), f32[8,8,1280]{2,1,0:T(8,128)S(1)}, u32[]{:S(2)}, u32[]{:S(2)}) async-start(f32[8,8,1280]{2,1,0:T(8,128)} %bitcast.35), calls=%async_computation.4 | async-start | bytes 655360 | tf_op jit(solution)/shard_map/all_to_all | solution.py:268

commit v5 on v4

--- a/solution.py
+++ b/solution.py
@@ -84,7 +84,7 @@
     def block(halves, row):
         return jnp.concatenate(
             [
-                jnp.concatenate([gathered[16 * m + row : 16 * m + row + 8] for m in (4 * j + i for i in halves)], axis=1)
+                jnp.concatenate([gathered[16 * m + row : 16 * m + row + 8] for m in (8 * i + j for i in halves)], axis=1)
                 for j in range(8)
             ],
             axis=0,
@@ -97,8 +97,11 @@
     own = jnp.concatenate(pred[:2], axis=1)
     energy = jnp.broadcast_to(row_squares(own), (64, 128))
     spread = [times(pred[b], same[b], NN) + times(pred[b + 1], before[b + 1], NN) for b in range(2)]
-    grad = times(jnp.concatenate(spread, axis=1), split(design()), NN)
-    return jnp.concatenate([back_grad, grad, energy], axis=1), own
+    left = jnp.concatenate(spread, axis=1)
+    parts = []
+    for k in range(back_grad.shape[1] // BLOCK):
+        parts.append(times(left, split(design(k)), NN))
+    return jnp.concatenate([back_grad, *parts, energy], axis=1), own
 
 
 def sum_pieces(pieces):
@@ -170,25 +173,25 @@
 
         copies = []
         copy(direction, dir_v, 0)
+        copy(gradient_prev, old_v, 1)
         for i in range(4):
-            copy(design.at[128 * i : 128 * i + 128], des_v.at[128 * i : 128 * i + 128], 1 + i)
-        copy(gradient_prev, old_v, 5)
+            copy(design.at[128 * i : 128 * i + 128], des_v.at[128 * i : 128 * i + 128], 2 + i)
         copy(whitening.at[:BLOCK], rim.at[:BLOCK], 6)
         copy(residual.at[:, :BLOCK], rim.at[BLOCK:], 7)
         copies[0].wait()
         left = dir_v[...]
-        for i in range(4):
-            copies[1 + i].wait()
-            part = times(left, split(des_v[128 * i : 128 * i + 128]), NT)
-            for j in range(8):
-                first = 9 * (4 * j + i)
-                rows_v[first : first + 8] = part[8 * j : 8 * j + 8]
-        copies[5].wait()
+        copies[1].wait()
         old = row_squares(old_v[...])
         for m in range(32):
             rows_v[9 * m + 8 : 9 * m + 9] = old
-        copy(rows_v, rows, 8)
-        for k in range(6, 9):
+        for i in range(4):
+            copies[2 + i].wait()
+            part = times(left, split(des_v[128 * i : 128 * i + 128]), NT)
+            for j in range(8):
+                first = 9 * (8 * i + j)
+                rows_v[first : first + 8] = part[8 * j : 8 * j + 8]
+            copy(rows_v.at[72 * i : 72 * i + 72], rows.at[72 * i : 72 * i + 72], 8 + i)
+        for k in range(6, 12):
             copies[k].wait()
 
     return pl.pallas_call(
@@ -204,7 +207,7 @@
             pltpu.VMEM(design.shape, F32),
             pltpu.VMEM(gradient_prev.shape, F32),
             pltpu.VMEM((9 * 32, 128), F32),
-            pltpu.SemaphoreType.DMA((9,)),
+            pltpu.SemaphoreType.DMA((12,)),
         ],
         compiler_params=LIMIT,
         name="predict",
@@ -241,13 +244,18 @@
 
 
 def project(gathered, bands, back_grad, design):
-    def kernel(gathered, b0, b1, b2, b3, back_grad, design, pieces, predicted, des_v, sem):
-        copy = pltpu.make_async_copy(design, des_v, sem)
-        copy.start()
-
-        def fetched():
-            copy.wait()
-            return des_v[...]
+    count = design.shape[1] // BLOCK
+
+    def kernel(gathered, b0, b1, b2, b3, back_grad, design, pieces, predicted, des_v, sems):
+        copies = []
+        for k in range(count):
+            cut = pl.ds(BLOCK * k, BLOCK)
+            copies.append(pltpu.make_async_copy(design.at[:, cut], des_v.at[:, cut], sems.at[k]))
+            copies[-1].start()
+
+        def fetched(k):
+            copies[k].wait()
+            return des_v[:, BLOCK * k : BLOCK * (k + 1)]
 
         pieces[...], predicted[...] = whiten_and_project(
             gathered[...], b0[...], b1[...], b2[...], b3[...], back_grad[...], fetched
@@ -258,7 +266,7 @@
         out_shape=[pltpu.VMEM((64, 2 * design.shape[1] + 128), F32), pltpu.VMEM((64, design.shape[0]), F32)],
         in_specs=[VMEM] * 6 + [HBM],
         out_specs=[VMEM] * 2,
-        scratch_shapes=[pltpu.VMEM(design.shape, F32), pltpu.SemaphoreType.DMA],
+        scratch_shapes=[pltpu.VMEM(design.shape, F32), pltpu.SemaphoreType.DMA((count,))],
         compiler_params=LIMIT,
         name="whiten_and_project",
     )(near(gathered), *[near(b) for b in bands], near(back_grad), far(design))
@@ -283,7 +291,7 @@
     pairs = []
     for t in range(blocks_t):
         for c in range(blocks_c):
-            to = t + 1 if c % 4 >= 2 else t - 1
+            to = t + 1 if c >= blocks_c // 2 else t - 1
             if 0 <= to < blocks_t:
                 pairs.append((t * blocks_c + c, to * blocks_c + c))
     rim_tile = lax.ppermute(tile, ("tm", "coef"), pairs)
@@ -292,7 +300,7 @@
     mine = run(sum_pieces, [(8, 2 * coefs + 128)], exchange(pieces, "tm", groups), close=(0,))
     other = lax.ppermute(mine, "tm", [(i, i ^ 2) for i in range(blocks_t)])
     grad, alpha, norms = run(
-        step_piece, [(8, coefs), (8, 128), (32, 128)], place, mine, other, old, keep=(0,), close=(1, 2, 3)
+        step_piece, [(8, coefs), (8, 128), (32, 128)], place, mine, other, old, keep=(0,), close=(1, 2, 3), away=(2,)
     )
     norms = exchange(norms, "coef")
     new_solution, new_residual = run(
@@ -306,7 +314,7 @@
         close=(0, 4),
         away=(0, 1),
     )
-    pieces = run(direction_piece, [(64, coefs)], place, norms, grad, old, direction, keep=(0, 4), close=(1, 2, 3), away=(0,))
+    pieces = run(direction_piece, [(64, coefs)], place, norms, grad, old, direction, keep=(0, 4), close=(1, 2, 3))
     return new_solution.T, new_residual.T, exchange(pieces, "tm", groups).T
 
 

time: 128 us -> 128 us (level)
  no operation moved by 1% of the time
where the time goes in v5:
time: 128 us
  blocking collectives  60.3 us (47%)
  waiting for transfers between devices  33 us (26%)
  starting transfers between devices  19.7 us (15%)
  Pallas kernels  13.5 us (11%)
    all_to_all x3, blocking collectives, exchange(): lax.all_to_all(rows, axis, 0, 0, axis_index_groups=groups, tiled=True)  60.3 us
    ppermute x1, waiting for transfers between devices, per_device(): rim = lax.ppermute(rim, 'tm', [(i + 1, i) for i in range(blocks_t - 1)])  14.1 us
    all_to_all x2, starting transfers between devices, exchange(): lax.all_to_all(rows, axis, 0, 0, axis_index_groups=groups, tiled=True)  9.97 us
    ppermute x1, waiting for transfers between devices, per_device(): rim_tile = lax.ppermute(tile, ('tm', 'coef'), pairs)  7.19 us
    all_to_all x2, waiting for transfers between devices, exchange(): lax.all_to_all(rows, axis, 0, 0, axis_index_groups=groups, tiled=True)  6.21 us
    ppermute x1, waiting for transfers between devices, per_device(): other = lax.ppermute(mine, 'tm', [(i, i ^ 2) for i in range(blocks_t)])  5.53 us
    ppermute x1, starting transfers between devices, per_device(): rim_tile = lax.ppermute(tile, ('tm', 'coef'), pairs)  4.18 us
    pallas_call x1, Pallas kernels, predict(): pl.pallas_call(kernel, out_shape=[pltpu.HBM((9 * 32, 128), F32), pltpu.VM...  3.93 us
  transfers between devices with their start and end apart: 5, of which 4 were waited for; matrix products, arithmetic and copies ran while one was open for 0% of the time, Pallas kernels for 3%

profile of v5, /device:TPU:1, one launch (start us, length us, event | category | flops | bytes accessed | tf_op | source)
XLA Modules:
  0.0 127.9 jit_solution(9621677426994823153)
XLA Ops:
  0.6 3.9 %predict.1 = (f32[288,128]{1,0:T(8,128)}, f32[320,256]{1,0:T(8,128)S(1)}) custom-call(f32[64,1280]{1,0:T(8,128)} %bitcast.21, f32[512,1280]{1,0:T(8,128)} %design.5, f32[64,1280]{1,0:T(8,128)} %bitcast.34, f32[512,256]{1,0:T(8,128)} %whitening.3, f32[64,512]{1,0:T(8,128)} %bitcast.25), custom_call_target="tpu_custom_call" | custom-call | tf_op jit(solution)/shard_map/predict/pallas_call | solution.py:197
  4.6 23.5 %all_to_all.54 = f32[32,1,1152]{2,1,0:T(1,128)S(1)} all-to-all(f32[32,1,1152]{2,1,0:T(1,128)} %bitcast.35), channel_id=1, replica_groups=mesh['tm'=16,'coef'=32] {'coef'}, dimensions={0} | all-to-all | bytes 294912 | tf_op jit(solution)/shard_map/all_to_all | solution.py:276
  28.1 4.2 %collective-permute-start = (f32[8,128]{1,0:T(8,128)S(1)}, f32[8,128]{1,0:T(8,128)S(1)}, u32[]{:S(2)}, u32[]{:S(2)}) collective-permute-start(f32[8,128]{1,0:T(8,128)S(1)} %get-tuple-element.20.refs_0_), channel_id=1, source_target_pairs={{16,48},{17,49},{18,50},{19,51},{20,52},{21,53},{22,54},{23,55},{2... | collective-permute-start | bytes 12296 | tf_op jit(solution)/shard_map/ppermute | solution.py:297
  32.3 7.2 %collective-permute-done.refs_1_ = f32[8,128]{1,0:T(8,128)S(1)} collective-permute-done((f32[8,128]{1,0:T(8,128)S(1)}, f32[8,128]{1,0:T(8,128)S(1)}, u32[]{:S(2)}, u32[]{:S(2)}) %collective-permute-start) | collective-permute-done | bytes 4128 | tf_op jit(solution)/shard_map/ppermute | solution.py:297
  39.5 0.7 shard_map.86
  40.2 3.9 %all-to-all-start.1 = ((f32[32,16,128]{2,1,0:T(8,128)}), f32[32,16,128]{2,1,0:T(8,128)S(1)}, u32[]{:S(2)}, u32[]{:S(2)}) async-start(f32[32,16,128]{2,1,0:T(8,128)} %bitcast.6), calls=%async_computation.1 | async-start | bytes 524288 | tf_op jit(solution)/shard_map/all_to_all | solution.py:276
  44.1 1.9 %collective-permute-start.1 = (f32[320,256]{1,0:T(8,128)S(1)}, f32[320,256]{1,0:T(8,128)S(1)}, u32[]{:S(2)}, u32[]{:S(2)}) collective-permute-start(f32[320,256]{1,0:T(8,128)S(1)} %get-tuple-element.21), channel_id=1, source_target_pairs={{32,0},{64,32},{96,64},{128,96},{160,128},{192,160},{224,192},{256... | collective-permute-start | bytes 983048 | tf_op jit(solution)/shard_map/ppermute | solution.py:288
  46.0 14.1 %collective-permute-done.1.rim = f32[320,256]{1,0:T(8,128)S(1)} collective-permute-done((f32[320,256]{1,0:T(8,128)S(1)}, f32[320,256]{1,0:T(8,128)S(1)}, u32[]{:S(2)}, u32[]{:S(2)}) %collective-permute-start.1) | collective-permute-done | bytes 327712 | tf_op jit(solution)/shard_map/ppermute | solution.py:288
  60.1 3.1 %band.1 = (bf16[3,256,256]{2,1,0:T(8,128)(2,1)S(1)}, bf16[3,256,256]{2,1,0:T(8,128)(2,1)S(1)}, bf16[3,256,256]{2,1,0:T(8,128)(2,1)S(1)}, bf16[3,256,256]{2,1,0:T(8,128)(2,1)S(1)}, f32[64,1280]{1,0:T(8,128)S(1)}) custom-call(f32[320,256]{1,0:T(8,128)S(1)} %collective-permute-done.1.rim, f32[512,256]{1,0:T(8,128)} %whitening.3, f32[64,512]{1,0:T(8,128)} %bitcast.26, ...), custom_call_target="tpu_custom_call" | custom-call | tf_op jit(solution)/shard_map/band/pallas_call | solution.py:235
  63.2 0.0 all-to-all-done.1
  63.2 0.0 copy-start
  63.3 3.1 %whiten_and_project.1 = (f32[64,2688]{1,0:T(8,128)S(1)}, f32[64,512]{1,0:T(8,128)S(1)}) custom-call(f32[512,128]{1,0:T(8,128)S(1)} %bitcast.28, bf16[3,256,256]{2,1,0:T(8,128)(2,1)S(1)} %get-tuple-element.22.b0, bf16[3,256,256]{2,1,0:T(8,128)(2,1)S(1)} %get-tuple-element.23.b1, bf16[3,256,256]{2,1,0:T(8,128)(2,1)S(1)} %get-tuple-element.24.b2, ...), custom_call_target="tpu_custom_call" | custom-call | tf_op jit(solution)/shard_map/whiten_and_project/pallas_call | solution.py:264
  66.4 0.0 copy-start.1
  66.4 0.0 copy-start.2
  66.4 16.4 %all_to_all.55 = f32[8,8,2688]{2,1,0:T(8,128)S(1)} all-to-all(f32[8,8,2688]{2,1,0:T(8,128)S(1)} %bitcast.29), channel_id=1, replica_groups={{0,32,128,160,256,288,384,416},{64,96,192,224,320,352,448,480},{1,33,12..., dimensions={0} | all-to-all | bytes 1376256 | tf_op jit(solution)/shard_map/all_to_all | solution.py:276
  82.8 3.6 %collective-permute-start.2 = (f32[8,2688]{1,0:T(8,128)S(1)}, f32[8,2688]{1,0:T(8,128)S(1)}, u32[]{:S(2)}, u32[]{:S(2)}) collective-permute-start(f32[8,2688]{1,0:T(8,128)S(1)} %shard_map.87.refs_1_), channel_id=1, source_target_pairs={{0,64},{32,96},{64,0},{96,32},{128,192},{160,224},{192,128},{224,1... | collective-permute-start | bytes 258056 | tf_op jit(solution)/shard_map/ppermute | solution.py:301
  86.4 5.5 %collective-permute-done.2.refs_2_ = f32[8,2688]{1,0:T(8,128)S(1)} collective-permute-done((f32[8,2688]{1,0:T(8,128)S(1)}, f32[8,2688]{1,0:T(8,128)S(1)}, u32[]{:S(2)}, u32[]{:S(2)}) %collective-permute-start.2) | collective-permute-done | bytes 86048 | tf_op jit(solution)/shard_map/ppermute | solution.py:301
  91.9 0.8 shard_map.88
  92.7 20.4 %all_to_all.56 = f32[32,1,128]{2,1,0:T(1,128)S(1)} all-to-all(f32[32,1,128]{2,1,0:T(1,128)} %bitcast.36), channel_id=1, replica_groups=mesh['tm'=16,'coef'=32] {'coef'}, dimensions={0} | all-to-all | bytes 32768 | tf_op jit(solution)/shard_map/all_to_all | solution.py:276
  113.1 0.0 copy-done
  113.1 0.8 shard_map.90
  114.0 6.1 %all-to-all-start.4 = ((f32[8,8,1280]{2,1,0:T(8,128)}), f32[8,8,1280]{2,1,0:T(8,128)S(1)}, u32[]{:S(2)}, u32[]{:S(2)}) async-start(f32[8,8,1280]{2,1,0:T(8,128)} %bitcast.16), calls=%async_computation.4 | async-start | bytes 655360 | tf_op jit(solution)/shard_map/all_to_all | solution.py:276
  120.1 0.0 copy-done.1
  120.1 0.0 copy-done.2
  120.1 0.9 shard_map.89
  121.0 6.2 %all-to-all-done.4 = f32[8,8,1280]{2,1,0:T(8,128)S(1)} async-done(((f32[8,8,1280]{2,1,0:T(8,128)}), f32[8,8,1280]{2,1,0:T(8,128)S(1)}, u32[]{:S(2)}, u32[]{:S(2)}) %all-to-all-start.4) | async-done | bytes 327712 | tf_op jit(solution)/shard_map/all_to_all | solution.py:276
  127.2 0.7 copy.12
  (2 shorter events, 0.1 us)
Async XLA Ops:
  28.1 11.4 %collective-permute-start = (f32[8,128]{1,0:T(8,128)S(1)}, f32[8,128]{1,0:T(8,128)S(1)}, u32[]{:S(2)}, u32[]{:S(2)}) collective-permute-start(f32[8,128]{1,0:T(8,128)S(1)} %get-tuple-element.20.refs_0_), channel_id=1, source_target_pairs={{16,48},{17,49},{18,50},{19,51},{20,52},{21,53},{22,54},{23,55},{2... | collective-permute-start | bytes 12296 | tf_op jit(solution)/shard_map/ppermute | solution.py:297
  40.2 23.0 %all-to-all-start.1 = ((f32[32,16,128]{2,1,0:T(8,128)}), f32[32,16,128]{2,1,0:T(8,128)S(1)}, u32[]{:S(2)}, u32[]{:S(2)}) async-start(f32[32,16,128]{2,1,0:T(8,128)} %bitcast.6), calls=%async_computation.1 | async-start | bytes 524288 | tf_op jit(solution)/shard_map/all_to_all | solution.py:276
  44.1 16.0 %collective-permute-start.1 = (f32[320,256]{1,0:T(8,128)S(1)}, f32[320,256]{1,0:T(8,128)S(1)}, u32[]{:S(2)}, u32[]{:S(2)}) collective-permute-start(f32[320,256]{1,0:T(8,128)S(1)} %get-tuple-element.21), channel_id=1, source_target_pairs={{32,0},{64,32},{96,64},{128,96},{160,128},{192,160},{224,192},{256... | collective-permute-start | bytes 983048 | tf_op jit(solution)/shard_map/ppermute | solution.py:288
  63.2 49.9 %copy-start = (f32[1280,64]{0,1:T(8,128)S(1)}, f32[1280,64]{0,1:T(8,128)}, u32[]{:S(2)}) copy-start(f32[1280,64]{0,1:T(8,128)} %param.9) | copy-start | bytes 983044
  66.4 53.7 %copy-start.1 = (f32[512,64]{0,1:T(8,128)S(1)}, f32[512,64]{0,1:T(8,128)}, u32[]{:S(2)}) copy-start(f32[512,64]{0,1:T(8,128)} %param.11) | copy-start | bytes 393220
  66.4 53.7 %copy-start.2 = (f32[1280,64]{0,1:T(8,128)S(1)}, f32[1280,64]{0,1:T(8,128)}, u32[]{:S(2)}) copy-start(f32[1280,64]{0,1:T(8,128)} %param.8) | copy-start | bytes 983044
  82.8 9.1 %collective-permute-start.2 = (f32[8,2688]{1,0:T(8,128)S(1)}, f32[8,2688]{1,0:T(8,128)S(1)}, u32[]{:S(2)}, u32[]{:S(2)}) collective-permute-start(f32[8,2688]{1,0:T(8,128)S(1)} %shard_map.87.refs_1_), channel_id=1, source_target_pairs={{0,64},{32,96},{64,0},{96,32},{128,192},{160,224},{192,128},{224,1... | collective-permute-start | bytes 258056 | tf_op jit(solution)/shard_map/ppermute | solution.py:301
  114.0 13.2 %all-to-all-start.4 = ((f32[8,8,1280]{2,1,0:T(8,128)}), f32[8,8,1280]{2,1,0:T(8,128)S(1)}, u32[]{:S(2)}, u32[]{:S(2)}) async-start(f32[8,8,1280]{2,1,0:T(8,128)} %bitcast.16), calls=%async_computation.4 | async-start | bytes 655360 | tf_op jit(solution)/shard_map/all_to_all | solution.py:276

commit v6 on v5

--- a/solution.py
+++ b/solution.py
@@ -165,8 +165,8 @@
 HBM, VMEM = pl.BlockSpec(memory_space=pltpu.HBM), pl.BlockSpec(memory_space=pltpu.VMEM)
 
 
-def predict(direction, design, gradient_prev, whitening, residual):
-    def kernel(direction, design, gradient_prev, whitening, residual, rows, rim, dir_v, des_v, old_v, rows_v, sems):
+def predict(direction, design, gradient_prev):
+    def kernel(direction, design, gradient_prev, rows, dir_v, des_v, old_v, rows_v, sems):
         def copy(source, target, k):
             copies.append(pltpu.make_async_copy(source, target, sems.at[k]))
             copies[-1].start()
@@ -176,8 +176,6 @@
         copy(gradient_prev, old_v, 1)
         for i in range(4):
             copy(design.at[128 * i : 128 * i + 128], des_v.at[128 * i : 128 * i + 128], 2 + i)
-        copy(whitening.at[:BLOCK], rim.at[:BLOCK], 6)
-        copy(residual.at[:, :BLOCK], rim.at[BLOCK:], 7)
         copies[0].wait()
         left = dir_v[...]
         copies[1].wait()
@@ -190,28 +188,47 @@
             for j in range(8):
                 first = 9 * (8 * i + j)
                 rows_v[first : first + 8] = part[8 * j : 8 * j + 8]
-            copy(rows_v.at[72 * i : 72 * i + 72], rows.at[72 * i : 72 * i + 72], 8 + i)
-        for k in range(6, 12):
+            copy(rows_v.at[72 * i : 72 * i + 72], rows.at[72 * i : 72 * i + 72], 6 + i)
+        for k in range(6, 10):
             copies[k].wait()
 
     return pl.pallas_call(
         kernel,
-        out_shape=[
-            pltpu.HBM((9 * 32, 128), F32),
-            pltpu.VMEM((BLOCK + 64, BLOCK), F32),
-        ],
-        in_specs=[HBM] * 5,
-        out_specs=[HBM, VMEM],
+        out_shape=pltpu.HBM((9 * 32, 128), F32),
+        in_specs=[HBM] * 3,
+        out_specs=HBM,
         scratch_shapes=[
             pltpu.VMEM(direction.shape, F32),
             pltpu.VMEM(design.shape, F32),
             pltpu.VMEM(gradient_prev.shape, F32),
             pltpu.VMEM((9 * 32, 128), F32),
-            pltpu.SemaphoreType.DMA((12,)),
+            pltpu.SemaphoreType.DMA((10,)),
         ],
         compiler_params=LIMIT,
         name="predict",
-    )(*[far(a) for a in (direction, design, gradient_prev, whitening, residual)])
+    )(far(direction), far(design), far(gradient_prev))
+
+
+def rim_rows(whitening, residual):
+    def kernel(whitening, residual, rim, sems):
+        copies = [
+            pltpu.make_async_copy(whitening.at[:BLOCK], rim.at[:BLOCK], sems.at[0]),
+            pltpu.make_async_copy(residual.at[:, :BLOCK], rim.at[BLOCK:], sems.at[1]),
+        ]
+        for copy in copies:
+            copy.start()
+        for copy in copies:
+            copy.wait()
+
+    return pl.pallas_call(
+        kernel,
+        out_shape=pltpu.VMEM((BLOCK + 64, BLOCK), F32),
+        in_specs=[HBM] * 2,
+        out_specs=VMEM,
+        scratch_shapes=[pltpu.SemaphoreType.DMA((2,))],
+        compiler_params=LIMIT,
+        name="rim_rows",
+    )(far(whitening), far(residual))
 
 
 def banded(whitening, rim, residual, design):
@@ -283,9 +300,9 @@
     groups = [[4 * x + 2 * z + k for x in range(4) for k in range(2)] for z in range(2)]
     t = lax.axis_index("tm").astype(jnp.int32)
     place = (lax.shift_right_logical(t, 2) * 2 + (t & 1))[None]
-    rows, rim = predict(direction, design, gradient_prev, whitening, residual)
+    rim = lax.ppermute(rim_rows(whitening, residual), "tm", [(i + 1, i) for i in range(blocks_t - 1)])
+    rows = predict(direction, design, gradient_prev)
     rows = exchange(rows.reshape(32, 9 * 128), "coef").reshape(9 * 32, 128)
-    rim = lax.ppermute(rim, "tm", [(i + 1, i) for i in range(blocks_t - 1)])
     *bands, back_grad = banded(whitening, rim, residual, design)
     tile, old = run(collect, [(8, 128), (8, 128)], rows, close=(0,))
     pairs = []

time: 128 us -> 129 us (level)
  starting transfers between devices: 19.7 us -> 23 us
  waiting for transfers between devices: 33 us -> 31 us
  blocking collectives: 60.3 us -> 58.7 us
    all_to_all x2, starting transfers between devices: 9.97 us -> 12.3 us  [exchange(): lax.all_to_all(rows, axis, 0, 0, axis_index_groups=groups, tiled=True)]
    all_to_all x3, blocking collectives: 60.3 us -> 58.7 us  [exchange(): lax.all_to_all(rows, axis, 0, 0, axis_index_groups=groups, tiled=True)]
    pallas_call x1 -> x2, Pallas kernels: 3.93 us -> 4.88 us  [the longest x1 3.91 us: predict(): pl.pallas_call(kernel, out_shape=pltpu.HBM((9 * 32, 128), F32), in_specs=...]
  transfers between devices with their start and end apart: 5 -> 5, of which waited for: 4 -> 4; matrix products, arithmetic and copies ran while one was open for 0% -> 0% of each run, Pallas kernels for 3% -> 4%
where the time goes in v6:
time: 129 us
  blocking collectives  58.7 us (46%)
  waiting for transfers between devices  31 us (24%)
  starting transfers between devices  23 us (18%)
  Pallas kernels  14.4 us (11%)
    all_to_all x3, blocking collectives, exchange(): lax.all_to_all(rows, axis, 0, 0, axis_index_groups=groups, tiled=True)  58.7 us
    ppermute x1, waiting for transfers between devices, per_device(): lax.ppermute(rim_rows(whitening, residual), 'tm', [(i + 1, i) for i in ra...  13.1 us
    all_to_all x2, starting transfers between devices, exchange(): lax.all_to_all(rows, axis, 0, 0, axis_index_groups=groups, tiled=True)  12.3 us
    ppermute x1, waiting for transfers between devices, per_device(): rim_tile = lax.ppermute(tile, ('tm', 'coef'), pairs)  7.19 us
    all_to_all x2, waiting for transfers between devices, exchange(): lax.all_to_all(rows, axis, 0, 0, axis_index_groups=groups, tiled=True)  6.21 us
    ppermute x1, starting transfers between devices, per_device(): other = lax.ppermute(mine, 'tm', [(i, i ^ 2) for i in range(blocks_t)])  4.57 us
    ppermute x1, waiting for transfers between devices, per_device(): other = lax.ppermute(mine, 'tm', [(i, i ^ 2) for i in range(blocks_t)])  4.55 us
    ppermute x1, starting transfers between devices, per_device(): rim_tile = lax.ppermute(tile, ('tm', 'coef'), pairs)  4.18 us
  transfers between devices with their start and end apart: 5, of which 4 were waited for; matrix products, arithmetic and copies ran while one was open for 0% of the time, Pallas kernels for 4%

profile of v6, /device:TPU:1, one launch (start us, length us, event | category | flops | bytes accessed | tf_op | source)
XLA Modules:
  0.0 128.7 jit_solution(11333944327798163698)
XLA Ops:
  0.6 3.9 %predict.1 = f32[288,128]{1,0:T(8,128)} custom-call(f32[64,1280]{1,0:T(8,128)} %bitcast.21, f32[512,1280]{1,0:T(8,128)} %design.5, f32[64,1280]{1,0:T(8,128)} %bitcast.35), custom_call_target="tpu_custom_call" | custom-call | tf_op jit(solution)/shard_map/predict/pallas_call | solution.py:195
  4.5 23.5 %all_to_all.54 = f32[32,1,1152]{2,1,0:T(1,128)S(1)} all-to-all(f32[32,1,1152]{2,1,0:T(1,128)} %bitcast.34), channel_id=1, replica_groups=mesh['tm'=16,'coef'=32] {'coef'}, dimensions={0} | all-to-all | bytes 294912 | tf_op jit(solution)/shard_map/all_to_all | solution.py:293
  28.1 4.2 %collective-permute-start = (f32[8,128]{1,0:T(8,128)S(1)}, f32[8,128]{1,0:T(8,128)S(1)}, u32[]{:S(2)}, u32[]{:S(2)}) collective-permute-start(f32[8,128]{1,0:T(8,128)S(1)} %get-tuple-element.17.refs_0_), channel_id=1, source_target_pairs={{16,48},{17,49},{18,50},{19,51},{20,52},{21,53},{22,54},{23,55},{2... | collective-permute-start | bytes 12296 | tf_op jit(solution)/shard_map/ppermute | solution.py:314
  32.3 7.2 %collective-permute-done.refs_1_ = f32[8,128]{1,0:T(8,128)S(1)} collective-permute-done((f32[8,128]{1,0:T(8,128)S(1)}, f32[8,128]{1,0:T(8,128)S(1)}, u32[]{:S(2)}, u32[]{:S(2)}) %collective-permute-start) | collective-permute-done | bytes 4128 | tf_op jit(solution)/shard_map/ppermute | solution.py:314
  39.5 0.7 shard_map.86
  40.2 3.9 %all-to-all-start.1 = ((f32[32,16,128]{2,1,0:T(8,128)}), f32[32,16,128]{2,1,0:T(8,128)S(1)}, u32[]{:S(2)}, u32[]{:S(2)}) async-start(f32[32,16,128]{2,1,0:T(8,128)} %bitcast.5), calls=%async_computation.1 | async-start | bytes 524288 | tf_op jit(solution)/shard_map/all_to_all | solution.py:293
  44.1 1.0 rim_rows.1
  45.1 1.9 %collective-permute-start.1 = (f32[320,256]{1,0:T(8,128)S(1)}, f32[320,256]{1,0:T(8,128)S(1)}, u32[]{:S(2)}, u32[]{:S(2)}) collective-permute-start(f32[320,256]{1,0:T(8,128)S(1)} %rim_rows.1), channel_id=1, source_target_pairs={{32,0},{64,32},{96,64},{128,96},{160,128},{192,160},{224,192},{256... | collective-permute-start | bytes 983048 | tf_op jit(solution)/shard_map/ppermute | solution.py:303
  47.0 13.1 %collective-permute-done.1.rim = f32[320,256]{1,0:T(8,128)S(1)} collective-permute-done((f32[320,256]{1,0:T(8,128)S(1)}, f32[320,256]{1,0:T(8,128)S(1)}, u32[]{:S(2)}, u32[]{:S(2)}) %collective-permute-start.1) | collective-permute-done | bytes 327712 | tf_op jit(solution)/shard_map/ppermute | solution.py:303
  60.1 3.1 %band.1 = (bf16[3,256,256]{2,1,0:T(8,128)(2,1)S(1)}, bf16[3,256,256]{2,1,0:T(8,128)(2,1)S(1)}, bf16[3,256,256]{2,1,0:T(8,128)(2,1)S(1)}, bf16[3,256,256]{2,1,0:T(8,128)(2,1)S(1)}, f32[64,1280]{1,0:T(8,128)S(1)}) custom-call(f32[320,256]{1,0:T(8,128)S(1)} %collective-permute-done.1.rim, f32[512,256]{1,0:T(8,128)} %whitening.3, f32[64,512]{1,0:T(8,128)} %bitcast.26, ...), custom_call_target="tpu_custom_call" | custom-call | tf_op jit(solution)/shard_map/band/pallas_call | solution.py:252
  63.2 0.0 all-to-all-done.1
  63.2 0.0 copy-start
  63.2 3.1 %whiten_and_project.1 = (f32[64,2688]{1,0:T(8,128)S(1)}, f32[64,512]{1,0:T(8,128)S(1)}) custom-call(f32[512,128]{1,0:T(8,128)S(1)} %bitcast.28, bf16[3,256,256]{2,1,0:T(8,128)(2,1)S(1)} %get-tuple-element.18.b0, bf16[3,256,256]{2,1,0:T(8,128)(2,1)S(1)} %get-tuple-element.19.b1, bf16[3,256,256]{2,1,0:T(8,128)(2,1)S(1)} %get-tuple-element.20.b2, ...), custom_call_target="tpu_custom_call" | custom-call | tf_op jit(solution)/shard_map/whiten_and_project/pallas_call | solution.py:281
  66.4 0.0 copy-start.1
  66.4 0.0 copy-start.2
  66.4 16.1 %all_to_all.55 = f32[8,8,2688]{2,1,0:T(8,128)S(1)} all-to-all(f32[8,8,2688]{2,1,0:T(8,128)S(1)} %bitcast.29), channel_id=1, replica_groups={{0,32,128,160,256,288,384,416},{64,96,192,224,320,352,448,480},{1,33,12..., dimensions={0} | all-to-all | bytes 1376256 | tf_op jit(solution)/shard_map/all_to_all | solution.py:293
  82.5 4.6 %collective-permute-start.2 = (f32[8,2688]{1,0:T(8,128)S(1)}, f32[8,2688]{1,0:T(8,128)S(1)}, u32[]{:S(2)}, u32[]{:S(2)}) collective-permute-start(f32[8,2688]{1,0:T(8,128)S(1)} %shard_map.87.refs_1_), channel_id=1, source_target_pairs={{0,64},{32,96},{64,0},{96,32},{128,192},{160,224},{192,128},{224,1... | collective-permute-start | bytes 258056 | tf_op jit(solution)/shard_map/ppermute | solution.py:318
  87.1 4.5 %collective-permute-done.2.refs_2_ = f32[8,2688]{1,0:T(8,128)S(1)} collective-permute-done((f32[8,2688]{1,0:T(8,128)S(1)}, f32[8,2688]{1,0:T(8,128)S(1)}, u32[]{:S(2)}, u32[]{:S(2)}) %collective-permute-start.2) | collective-permute-done | bytes 86048 | tf_op jit(solution)/shard_map/ppermute | solution.py:318
  91.7 0.8 shard_map.88
  92.5 19.1 %all_to_all.56 = f32[32,1,128]{2,1,0:T(1,128)S(1)} all-to-all(f32[32,1,128]{2,1,0:T(1,128)} %bitcast.36), channel_id=1, replica_groups=mesh['tm'=16,'coef'=32] {'coef'}, dimensions={0} | all-to-all | bytes 32768 | tf_op jit(solution)/shard_map/all_to_all | solution.py:293
  111.6 0.0 copy-done
  111.6 0.8 shard_map.90
  112.4 8.4 %all-to-all-start.4 = ((f32[8,8,1280]{2,1,0:T(8,128)}), f32[8,8,1280]{2,1,0:T(8,128)S(1)}, u32[]{:S(2)}, u32[]{:S(2)}) async-start(f32[8,8,1280]{2,1,0:T(8,128)} %bitcast.16), calls=%async_computation.4 | async-start | bytes 655360 | tf_op jit(solution)/shard_map/all_to_all | solution.py:293
  120.8 0.0 copy-done.1
  120.8 0.0 copy-done.2
  120.8 0.9 shard_map.89
  121.7 6.2 %all-to-all-done.4 = f32[8,8,1280]{2,1,0:T(8,128)S(1)} async-done(((f32[8,8,1280]{2,1,0:T(8,128)}), f32[8,8,1280]{2,1,0:T(8,128)S(1)}, u32[]{:S(2)}, u32[]{:S(2)}) %all-to-all-start.4) | async-done | bytes 327712 | tf_op jit(solution)/shard_map/all_to_all | solution.py:293
  127.9 0.7 copy.12
  (2 shorter events, 0.1 us)
Async XLA Ops:
  28.1 11.4 %collective-permute-start = (f32[8,128]{1,0:T(8,128)S(1)}, f32[8,128]{1,0:T(8,128)S(1)}, u32[]{:S(2)}, u32[]{:S(2)}) collective-permute-start(f32[8,128]{1,0:T(8,128)S(1)} %get-tuple-element.17.refs_0_), channel_id=1, source_target_pairs={{16,48},{17,49},{18,50},{19,51},{20,52},{21,53},{22,54},{23,55},{2... | collective-permute-start | bytes 12296 | tf_op jit(solution)/shard_map/ppermute | solution.py:314
  40.2 23.0 %all-to-all-start.1 = ((f32[32,16,128]{2,1,0:T(8,128)}), f32[32,16,128]{2,1,0:T(8,128)S(1)}, u32[]{:S(2)}, u32[]{:S(2)}) async-start(f32[32,16,128]{2,1,0:T(8,128)} %bitcast.5), calls=%async_computation.1 | async-start | bytes 524288 | tf_op jit(solution)/shard_map/all_to_all | solution.py:293
  45.1 15.0 %collective-permute-start.1 = (f32[320,256]{1,0:T(8,128)S(1)}, f32[320,256]{1,0:T(8,128)S(1)}, u32[]{:S(2)}, u32[]{:S(2)}) collective-permute-start(f32[320,256]{1,0:T(8,128)S(1)} %rim_rows.1), channel_id=1, source_target_pairs={{32,0},{64,32},{96,64},{128,96},{160,128},{192,160},{224,192},{256... | collective-permute-start | bytes 983048 | tf_op jit(solution)/shard_map/ppermute | solution.py:303
  63.2 48.4 %copy-start = (f32[1280,64]{0,1:T(8,128)S(1)}, f32[1280,64]{0,1:T(8,128)}, u32[]{:S(2)}) copy-start(f32[1280,64]{0,1:T(8,128)} %param.9) | copy-start | bytes 983044
  66.4 54.5 %copy-start.1 = (f32[512,64]{0,1:T(8,128)S(1)}, f32[512,64]{0,1:T(8,128)}, u32[]{:S(2)}) copy-start(f32[512,64]{0,1:T(8,128)} %param.11) | copy-start | bytes 393220
  66.4 54.5 %copy-start.2 = (f32[1280,64]{0,1:T(8,128)S(1)}, f32[1280,64]{0,1:T(8,128)}, u32[]{:S(2)}) copy-start(f32[1280,64]{0,1:T(8,128)} %param.8) | copy-start | bytes 983044
  82.5 9.1 %collective-permute-start.2 = (f32[8,2688]{1,0:T(8,128)S(1)}, f32[8,2688]{1,0:T(8,128)S(1)}, u32[]{:S(2)}, u32[]{:S(2)}) collective-permute-start(f32[8,2688]{1,0:T(8,128)S(1)} %shard_map.87.refs_1_), channel_id=1, source_target_pairs={{0,64},{32,96},{64,0},{96,32},{128,192},{160,224},{192,128},{224,1... | collective-permute-start | bytes 258056 | tf_op jit(solution)/shard_map/ppermute | solution.py:318
  112.4 15.5 %all-to-all-start.4 = ((f32[8,8,1280]{2,1,0:T(8,128)}), f32[8,8,1280]{2,1,0:T(8,128)S(1)}, u32[]{:S(2)}, u32[]{:S(2)}) async-start(f32[8,8,1280]{2,1,0:T(8,128)} %bitcast.16), calls=%async_computation.4 | async-start | bytes 655360 | tf_op jit(solution)/shard_map/all_to_all | solution.py:293
